TPU v7x, 128 devices: a whole 4x4x4 slice. The times are simulated.
128 devices in a mesh: sky: 16 (over y, x), tm: 8 (over z, core).
Axes of the slice: x: 4, y: 4, z: 4, core: 2. Of those that a mesh axis runs over, the one named last changes fastest.
Arguments:
- reference_spectra: float32 [524288, 64], P('sky'), may hold values from -6 to 6
- observed: float32 [16, 131072, 64], P('sky', 'tm'), may hold values from -6 to 6
- epoch_time: float32 [16, 131072], P('sky', 'tm'), may hold values from -1 to 1
- owner: int32 [16, 131072, 1], P('sky', 'tm'), may hold values from 0 to 15; in each aligned block of 16384 rows (0 to 16383, 16384 to 32767, ..., all dimensions but the last counted through in order) at most 4096 rows name the same one
- source_row: int32 [16, 131072], P('sky', 'tm'), may hold values from 0 to 32767
- unit: int32 [16, 131072, 1], P('sky', 'tm'), may hold values from 0 to 31, as said below
Outputs:
- factor: float32 [16, 32, 192, 192], P('sky', 'tm')
Inputs may be any that keep to these rules, and one draw needn't show every extreme that they name: `owner`: among the epochs of one device, at most 4096 name any one sky region, and on some device one region is named by exactly 4096. Among the epochs of one device, every unit has at least 256 and at most 1024 of them; some unit has exactly 256 and some unit exactly 1024.
All inputs are finite; a program needn't handle non-finite values.
Results may differ from a plain program's by a relative error of at most 0.0003.
Values sent between devices are 32-bit elements; how exact they have to be, the bound alone decides.
A program may use at most 256 MiB of HBM per device.

v0:
```python
import jax
import jax.numpy as jnp
from jax import lax
from jax.sharding import PartitionSpec as P

UNITS = 32
CAP = 4096
UCAP = 1024


def slot_index(labels, label_count, capacity):
    onehot = (labels[:, None] == jnp.arange(label_count, dtype=jnp.int32)[None, :]).astype(
        jnp.int32
    )
    ranking = jnp.sum(jnp.cumsum(onehot, axis=0) * onehot, axis=1) - 1
    return labels * capacity + ranking


def upper_factor(matrices):
    return jnp.swapaxes(jnp.linalg.cholesky(matrices), 1, 2)


def per_device(reference_spectra, observed, epoch_time, owner, source_row, unit):
    observed_local = observed[0]
    times_local = epoch_time[0]
    owners = owner[0, :, 0]
    src_rows = source_row[0]
    unit_ids = unit[0, :, 0]
    rows_dev = observed_local.shape[0]
    sky_count = lax.axis_size("sky")
    time_count = lax.axis_size("tm")
    coeff_count = reference_spectra.shape[1]
    placing = slot_index(owners, sky_count, CAP)
    requests = jnp.zeros((sky_count * CAP,), jnp.int32).at[placing].set(src_rows)
    requests = requests.reshape(sky_count, CAP)
    fetched = jnp.take(
        reference_spectra,
        lax.all_to_all(requests, "sky", split_axis=0, concat_axis=0, tiled=True),
        axis=0,
    )
    replies = lax.all_to_all(fetched, "sky", split_axis=0, concat_axis=0, tiled=True)
    ref_rows = replies.reshape(sky_count * CAP, coeff_count)[placing]
    row_scale = (UNITS / (rows_dev * time_count)) ** 0.5
    design = (
        jnp.concatenate([ref_rows, times_local[:, None] * ref_rows, observed_local], axis=1)
        * row_scale
    )
    column_count = design.shape[1]
    unit_place = slot_index(unit_ids, UNITS, UCAP)
    buffer = jnp.zeros((UNITS * UCAP, column_count), design.dtype).at[unit_place].set(design)
    buffer = buffer.reshape(UNITS, UCAP, column_count)
    local_gram = jnp.einsum("ucp,ucq->upq", buffer, buffer, precision=lax.Precision.HIGHEST)
    shared_gram = lax.psum_scatter(local_gram, "tm", scatter_dimension=0, tiled=True)
    own_part = upper_factor(shared_gram)
    return own_part[None]


def solution(mesh):
    placed = (
        P("sky", None),
        P("sky", "tm", None),
        P("sky", "tm"),
        P("sky", "tm", None),
        P("sky", "tm"),
        P("sky", "tm", None),
    )
    return jax.shard_map(
        per_device,
        mesh=mesh,
        in_specs=placed,
        out_specs=P("sky", "tm", None, None),
        check_vma=False,
    )
```

profile of v0, /device:TPU:1, one launch (start us, length us, event | category | flops | bytes accessed | tf_op | source)
XLA Modules:
  0.0 1016.4 jit_solution(14179878302768627140)
XLA Ops:
  6.5 0.9 copy.57
  7.5 0.2 fusion.13
  7.6 0.3 reduce-window.19
  7.9 0.1 broadcast_add_fusion.1
  8.0 0.4 copy.58
  8.4 1.6 fusion.12
  10.1 0.9 compare_select_fusion.2
  11.0 61.2 %scatter_custom_fusion = s32[65536]{0:T(1024)} fusion(s32[16384]{0:T(1024)S(1)} %bitcast.90, s32[16384]{0:T(1024)} %bitcast.96, s32[]{:T(128)} %constant.107.clone.1), kind=kCustom, calls=%fused_computation.49 | custom fusion | bytes 262656 | tf_op jit(solution)/shard_map/scatter | solution.py:34
  72.3 7.6 all-to-all-start
  79.8 12.2 %copy.59 = f32[32768,64]{1,0:T(8,128)} copy(f32[32768,64]{0,1:T(8,128)} %param.6) | data formatting | bytes 16777216 | tf_op args[0]
  92.1 0.0 all-to-all-done
  92.1 0.3 compare_select_fusion
  92.4 221.3 %gather_fusion = f32[65536,64]{1,0:T(8,128)} fusion(f32[32768,64]{1,0:T(8,128)} %copy.59, s32[65536]{0:T(1024)S(1)} %broadcast_clamp_fusion), kind=kCustom, calls=%fused_computation | custom fusion | bytes 33816576 | tf_op jit(solution)/shard_map/jit(_take)/gather | solution.py:36
  313.7 24.5 %copy.60 = f32[16,4096,64]{1,2,0:T(8,128)} copy(f32[16,4096,64]{2,1,0:T(8,128)} %bitcast.81) | data formatting | bytes 33554432 | tf_op jit(solution)/shard_map/jit(_take)/gather | solution.py:36
  338.2 0.2 compare_and_fusion
  338.4 12.1 %broadcast_select_fusion = f32[16,4096,64]{1,2,0:T(8,128)} fusion(f32[16,4096,64]{1,2,0:T(8,128)} %copy.60, pred[16,4096]{1,0:T(8,128)(4,1)S(1)} %compare_and_fusion), kind=kLoop, calls=%fused_computation.12 | loop fusion | flops 4194304 | bytes 33619968 | tf_op jit(solution)/shard_map/jit(_take)/select_n | solution.py:36
  350.5 6.8 all-to-all-start.1
  357.3 0.5 reduce-scatter.2.cloned.1.call-start
  357.9 0.0 copy-done
  357.9 0.1 copy.55
  358.0 0.3 fusion.9
  358.3 0.3 reduce-window.15
  358.6 1.6 broadcast_add_fusion
  360.2 2.0 copy.56
  362.2 6.9 copy.62
  369.0 1.7 fusion.8
  370.8 0.1 compare_select_fusion.3
  370.9 232.5 %all-to-all-done.1 = f32[16,4096,64]{1,2,0:T(8,128)} async-done(((f32[16,4096,64]{1,2,0:T(8,128)}), f32[16,4096,64]{1,2,0:T(8,128)}, u32[]{:S(2)}, u32[]{:S(2)}) %all-to-all-start.1) | async-done | bytes 16777248 | tf_op jit(solution)/shard_map/all_to_all | solution.py:41
  603.4 22.9 %copy.61 = f32[16,4096,64]{2,1,0:T(8,128)} copy(f32[16,4096,64]{1,2,0:T(8,128)} %all-to-all-done.1) | data formatting | bytes 33554432 | tf_op jit(solution)/shard_map/all_to_all | solution.py:41
  626.3 64.9 %gather_fusion.1 = f32[16384,64]{1,0:T(8,128)} fusion(f32[65536,64]{1,0:T(8,128)} %bitcast.80, s32[16384]{0:T(1024)S(1)} %broadcast_clamp_fusion.1), kind=kCustom, calls=%fused_computation.1 | custom fusion | bytes 8454144 | tf_op jit(solution)/shard_map/gather | solution.py:42
  691.2 7.9 broadcast_multiply_fusion
  699.1 87.9 %scatter_custom_fusion.1 = f32[32768,192]{1,0:T(8,128)} fusion(s32[16384]{0:T(1024)S(1)} %bitcast.95, f32[16384,64]{1,0:T(8,128)} %bitcast.82, f32[]{:T(128)} %constant.125, f32[16384,64]{1,0:T(8,128)} %broadcast_multiply_fusion, f32[16384,64]{1,0:T(8,128)} %gather_fusion.1, f32[]{:T(128)} %constant.105.clone.1, f32[]{:T(128)} %constant.114.clone.1), kind=kCustom, calls=%fused_computation.5 | custom fusion | flops 9437184 | bytes 37748748 | tf_op jit(solution)/shard_map/scatter | solution.py:50
  787.0 63.1 %fusion.23 = f32[32,192,192]{1,2,0:T(8,128)} fusion(f32[32,1024,192]{2,1,0:T(8,128)} %bitcast.79), kind=kOutput, calls=%fused_computation.65 | convolution fusion | flops 14495514624 | bytes 29884416 | tf_op jit(solution)/shard_map/ucp,ucq->upq/dot_general | solution.py:52
  850.1 0.0 reduce-scatter.2.cloned.1.call-update
  850.2 44.2 %reduce-scatter.2.cloned.1.call-done = f32[4,192,192]{1,2,0:T(8,128)} async-done(((f32[32,192,192]{1,2,0:T(8,128)}), f32[4,192,192]{1,2,0:T(8,128)}) %reduce-scatter.2.cloned.1.call-update) | async-done | bytes 589840 | tf_op jit(solution)/shard_map/reduce_scatter | solution.py:53
  894.4 1.4 copy.67
  895.9 1.2 fusion.16
  897.1 46.9 %custom-call.13 = f32[4,128,128]{2,1,0:T(8,128)S(1)} custom-call(f32[4,128,128]{2,1,0:T(8,128)S(1)} %cholesky.129), custom_call_target="Cholesky" | custom-call | tf_op jit(solution)/shard_map/jit(cholesky)/cholesky | solution.py:20
  944.0 0.1 cholesky.124
  944.1 0.1 select_reduce_fusion
  944.2 39.3 %custom-call.14 = f32[4,1,128,128]{2,3,1,0:T(8,128)S(1)} custom-call(f32[4,1,128,128]{3,2,1,0:T(8,128)S(1)} %get-tuple-element.6), custom_call_target="InvertDiagBlocksLowerTriangular" | custom-call | tf_op jit(solution)/shard_map/jit(cholesky)/cholesky | solution.py:20
  983.5 0.4 constant_dynamic-update-slice_fusion.1
  983.8 0.3 convolution_subtract_fusion
  984.2 23.5 %custom-call.15 = f32[4,64,64]{2,1,0:T(8,128)S(1)} custom-call(f32[4,64,64]{2,1,0:T(8,128)S(1)} %convolution_subtract_fusion), custom_call_target="Cholesky" | custom-call | tf_op jit(solution)/shard_map/jit(cholesky)/cholesky | solution.py:20
  1007.7 0.1 compare_reduce_fusion
  1007.8 0.1 compare_reduce_fusion.1
  1007.9 0.1 select_bitcast_fusion
  1008.1 1.2 copy.69
  (17 shorter events, 0.2 us)
Async XLA Ops:
  72.3 19.8 %all-to-all-start = ((s32[16,1,4096]{2,1,0:T(1,128)}), s32[16,1,4096]{2,1,0:T(1,128)S(1)}, u32[]{:S(2)}, u32[]{:S(2)}) async-start(s32[16,1,4096]{2,1,0:T(1,128)} %bitcast.15), calls=%async_computation | async-start | bytes 524288 | tf_op jit(solution)/shard_map/all_to_all | solution.py:38
  350.5 7.4 copy-start
  350.5 252.9 %all-to-all-start.1 = ((f32[16,4096,64]{1,2,0:T(8,128)}), f32[16,4096,64]{1,2,0:T(8,128)}, u32[]{:S(2)}, u32[]{:S(2)}) async-start(f32[16,4096,64]{1,2,0:T(8,128)} %broadcast_select_fusion), calls=%async_computation.1 | async-start | bytes 33554432 | tf_op jit(solution)/shard_map/all_to_all | solution.py:41
  357.3 537.1 %reduce-scatter.2.cloned.1.call-start = ((), (), s32[]{:S(2)}) async-start(), calls=%async_computation.3 | async-start | bytes 7077888 | tf_op jit(solution)/shard_map/reduce_scatter | solution.py:53
  626.3 64.9 %copy-start.1 = (f32[1,16384]{1,0:T(1,128)S(1)}, f32[1,16384]{1,0:T(1,128)}, u32[]{:S(2)}) copy-start(f32[1,16384]{1,0:T(1,128)} %param.8) | copy-start | bytes 196612
Sparse Core Ops, SparseCore 0:
  850.2 44.1 reduce-scatter.1
where the time goes:
time: 1020 us
  local copies, waits for them, and re-layouts  420 us (41%)
  waiting for transfers between devices  277 us (27%)
  other arithmetic  227 us (22%)
  matrix products  63.8 us (6%)
  starting transfers between devices  14.9 us (1%)
  between operations  13.9 us (1%)
    gather x2, local copies, waits for them, and re-layouts, per_device(): jnp.take(reference_spectra, lax.all_to_all(requests, 'sky', split_axis=0,...  246 us
    all_to_all x1, waiting for transfers between devices, per_device(): lax.all_to_all(fetched, 'sky', split_axis=0, concat_axis=0, tiled=True)  233 us
    another operation x10, other arithmetic, upper_factor(): return jnp.swapaxes(jnp.linalg.cholesky(matrices), 1, 2)  110 us
    scatter x1, other arithmetic, per_device(): jnp.zeros((UNITS * UCAP, column_count), design.dtype).at[unit_place]  87.9 us
    gather x1, local copies, waits for them, and re-layouts, per_device(): ref_rows = replies.reshape(sky_count * CAP, coeff_count)[placing]  64.9 us
    dot_general x1, matrix products, per_device(): jnp.einsum('ucp,ucq->upq', buffer, buffer, precision=lax.Precision.HIGHEST)  63.1 us
    scatter x1, local copies, waits for them, and re-layouts, per_device(): jnp.zeros((sky_count * CAP,), jnp.int32).at[placing].set(src_rows)  61.2 us
    reduce_scatter x1, waiting for transfers between devices, per_device(): lax.psum_scatter(local_gram, 'tm', scatter_dimension=0, tiled=True)  44.2 us
  transfers between devices with their start and end apart: 3, of which 2 were waited for; matrix products, arithmetic and copies ran while one was open for 2% of the time, Pallas kernels for 0%

commit v1 on v0

v1 whole, which is shorter than its diff:
```python
import functools

import jax
import jax.numpy as jnp
from jax import lax
from jax.experimental import pallas as pl
from jax.experimental.pallas import tpu as pltpu
from jax.sharding import PartitionSpec as P

UNITS = 32
COEFFS = 64
UCAP = 1024
SKY = 16
TM = 8
DEVS = SKY * TM
E_DEV = 16384
STRIPE = 256
SLOTS = 192
HALF = SLOTS // 2
LINES = DEVS * HALF
BLOCK = 256
DUMP = UNITS * UCAP
F32 = jnp.float32
BF16 = jnp.bfloat16
I32 = jnp.int32


def dot(a, b, dims, precision=None):
    return lax.dot_general(a, b, (dims, ((), ())), precision=precision, preferred_element_type=F32)


def route_kernel(round_ref, owner_ref, row_ref, unit_ref, req_ref, slot_ref, place_ref, count_ref, acc_ref):
    first = round_ref[0] * SLOTS
    tri_row = lax.broadcasted_iota(I32, (BLOCK, BLOCK + 128), 0)
    tri_col = lax.broadcasted_iota(I32, (BLOCK, BLOCK + 128), 1)
    before = ((tri_row < tri_col) | (tri_col >= BLOCK)).astype(BF16)
    peers = lax.broadcasted_iota(I32, (DEVS, BLOCK), 0)
    units = lax.broadcasted_iota(I32, (UNITS, BLOCK), 0)
    ranks = lax.broadcasted_iota(I32, (SLOTS, BLOCK), 0)
    acc_ref[...] = jnp.zeros_like(acc_ref)

    def pair(ref, b):
        return jnp.concatenate([ref[pl.ds(2 * b, 1), :], ref[pl.ds(2 * b + 1, 1), :]], axis=1)

    def wide(base):
        return jnp.concatenate([base, base], axis=1)

    def step(b, carry):
        base, unit_base = carry
        owner, row, unit = pair(owner_ref, b), pair(row_ref, b), pair(unit_ref, b)
        stripe = row >> 8
        peer = ((stripe & (SKY - 1)) << 3) + (stripe >> 4)
        local = (owner << 8) + (row & (STRIPE - 1))
        hot = peers == peer
        ahead = dot(hot.astype(BF16), before, ((1,), (0,)))
        rank = jnp.sum(jnp.where(hot, ahead[:, :BLOCK] + wide(base), 0.0), axis=0, keepdims=True)
        rank = rank.astype(I32) - first
        active = (rank >= 0) & (rank < SLOTS)
        upper = jnp.where(rank >= HALF, 1, 0)
        slot = upper * LINES + peer * HALF + rank - upper * HALF
        slot = jnp.where(active, slot, 0)
        high = (local >> 6).astype(F32)
        low = (local & 63).astype(F32)
        values = jnp.concatenate([jnp.where(hot, high, 0.0), jnp.where(hot, low, 0.0)], axis=0).astype(BF16)
        put = (ranks == rank).astype(BF16)
        acc_ref[...] += dot(values, put, ((1,), (1,)))
        mine = (units == unit) & active
        unit_ahead = dot(mine.astype(BF16), before, ((1,), (0,)))
        unit_rank = jnp.sum(jnp.where(mine, unit_ahead[:, :BLOCK] + wide(unit_base), 0.0), axis=0, keepdims=True)
        place = jnp.where(active, unit * UCAP + unit_rank.astype(I32), DUMP)
        for half in range(2):
            lanes = slice(half * 128, half * 128 + 128)
            slot_ref[pl.ds(2 * b + half, 1), :] = slot[:, lanes]
            place_ref[pl.ds(2 * b + half, 1), :] = place[:, lanes]
        return base + ahead[:, BLOCK:], unit_base + unit_ahead[:, BLOCK:]

    start = (jnp.zeros((DEVS, 128), F32), jnp.zeros((UNITS, 128), F32))
    base, unit_base = lax.fori_loop(0, E_DEV // BLOCK, step, start, unroll=4)
    count_ref[...] = unit_base.astype(I32)
    more = (jnp.max(base).astype(I32) > first + SLOTS).astype(I32)
    req_ref[:, 0:128] = (acc_ref[0:DEVS, 0:128] * 64.0 + acc_ref[DEVS:, 0:128]).astype(I32)
    tail = (acc_ref[0:DEVS, 128:] * 64.0 + acc_ref[DEVS:, 128:]).astype(I32)
    req_ref[:, 128:] = jnp.concatenate([tail, jnp.zeros((DEVS, 256 - SLOTS), I32) + more], axis=1)


def route(number, owner, row, unit):
    vmem = pl.BlockSpec(memory_space=pltpu.VMEM)
    return pl.pallas_call(
        route_kernel,
        out_shape=(
            jax.ShapeDtypeStruct((DEVS, 256), I32),
            jax.ShapeDtypeStruct((128, 128), I32),
            jax.ShapeDtypeStruct((128, 128), I32),
            jax.ShapeDtypeStruct((UNITS, 128), I32),
        ),
        in_specs=[pl.BlockSpec(memory_space=pltpu.SMEM), vmem, vmem, vmem],
        out_specs=(vmem,) * 4,
        scratch_shapes=[pltpu.VMEM((2 * DEVS, SLOTS), F32)],
        name="route",
    )(number, owner, row, unit)


PEERS_STEP = 16


def serve_kernel(req_ref, tab_ref, out_ref, rows_ref):
    step = pl.program_id(0)

    @pl.when(step == 0)
    def _():
        for region in range(SKY):
            block = tab_ref[region]
            rows_ref[region * STRIPE : (region + 1) * STRIPE, :] = jnp.concatenate([block, block], axis=0).T

    left = lax.broadcasted_iota(I32, (1, 128), 1) < COEFFS

    def peer_rows(k, _):
        peer = step * PEERS_STEP + k
        for j in range(HALF):
            a = req_ref[peer, j]
            b = req_ref[peer, j + HALF]
            out_ref[k, j : j + 1, :] = jnp.where(left, rows_ref[pl.ds(a, 1), :], rows_ref[pl.ds(b, 1), :])
        return _

    lax.fori_loop(0, PEERS_STEP, peer_rows, 0)


def serve(requests, table):
    return pl.pallas_call(
        serve_kernel,
        grid=(DEVS // PEERS_STEP,),
        out_shape=jax.ShapeDtypeStruct((DEVS, HALF, 128), F32),
        in_specs=[
            pl.BlockSpec(memory_space=pltpu.SMEM),
            pl.BlockSpec((SKY, COEFFS, STRIPE), lambda i: (0, 0, 0), pipeline_mode=pl.Buffered(1)),
        ],
        out_specs=pl.BlockSpec((PEERS_STEP, HALF, 128), lambda i: (i, 0, 0)),
        scratch_shapes=[pltpu.VMEM((SKY * STRIPE, 128), F32)],
        name="serve",
    )(requests, table)


JOIN_STEPS = 8
JOIN_BLOCKS = 128 // JOIN_STEPS


def join_kernel(scale, slot_ref, place_ref, count_ref, time_ref, obs_ref, reply_ref, old_ref, out_ref,
                rows_ref, x0_ref, x1_ref, block_ref, sums_ref, sem):
    step = pl.program_id(0)

    @pl.when(step == 0)
    def _():
        copy = pltpu.make_async_copy(reply_ref, rows_ref.at[pl.ds(0, LINES), :], sem)
        copy.start()
        copy.wait()

        def turn(i, _):
            at = pl.multiple_of(i * 256, 256)
            rows_ref[pl.ds(LINES + at, 256), :] = pltpu.roll(rows_ref[pl.ds(at, 256), :], COEFFS, 1)
            return _

        lax.fori_loop(0, LINES // 256, turn, 0)

    left = lax.broadcasted_iota(I32, (1, 128), 1) < COEFFS

    def place_block(k, _):
        b = step * JOIN_BLOCKS + k
        at = pl.multiple_of(k * 128, 128)
        times = jnp.broadcast_to(time_ref[pl.ds(b, 1), :], (COEFFS, 128))
        block_ref[...] = jnp.concatenate([times, obs_ref[:, pl.ds(at, 128)]], axis=0).T
        for j in range(128):
            s = slot_ref[b, j]
            p = place_ref[b, j]
            r = rows_ref[pl.ds(s, 1), :]
            o = block_ref[j : j + 1, :]
            x0_ref[pl.ds(p, 1), :] = jnp.where(left, r, o)
            x1_ref[pl.ds(p, 1), :] = r * o
        return _

    lax.fori_loop(0, JOIN_BLOCKS, place_block, 0)

    @pl.when(step == JOIN_STEPS - 1)
    def _():
        def unit_gram(u, _):
            count = count_ref[u, 0]
            sums_ref[...] = jnp.zeros_like(sums_ref)

            def add(i, _):
                at = pl.multiple_of(u * UCAP + i * 256, 256)
                x = jnp.concatenate([x0_ref[pl.ds(at, 256), :], x1_ref[pl.ds(at, 256), :]], axis=1)
                rows = lax.broadcasted_iota(I32, (256, 256), 0) + i * 256
                x = jnp.where(rows < count, x, 0.0)
                high = x.astype(BF16)
                low = (x - high.astype(F32)).astype(BF16)
                sums_ref[...] += dot(high, jnp.concatenate([high, low], axis=1), ((0,), (0,)))
                return _

            lax.fori_loop(0, (count + 255) // 256, add, 0)
            cross = sums_ref[:, 256:]
            gram = (sums_ref[:, :256] + cross + cross.T) * scale
            turned = pltpu.roll(gram, COEFFS, 1)
            ref = slice(0, 64)
            obs = slice(64, 128)
            tim = slice(128, 192)
            out_ref[u, :, 0:128] = old_ref[u, :, 0:128] + jnp.where(left, gram[ref, 0:128], turned[ref, 128:256])
            out_ref[u, :, 128:256] = old_ref[u, :, 128:256] + jnp.where(left, turned[ref, 128:256], turned[tim, 128:256])
            out_ref[u, :, 256:384] = old_ref[u, :, 256:384] + jnp.where(left, turned[tim, 128:256], gram[obs, 0:128])
            return _

        lax.fori_loop(0, UNITS, unit_gram, 0)


def join(slot, place, count, times, obs, reply, old, scale):
    smem = pl.BlockSpec(memory_space=pltpu.SMEM)
    once = functools.partial(pl.BlockSpec, pipeline_mode=pl.Buffered(1))
    return pl.pallas_call(
        functools.partial(join_kernel, scale),
        grid=(JOIN_STEPS,),
        out_shape=jax.ShapeDtypeStruct((UNITS, COEFFS, 384), F32),
        in_specs=[
            smem,
            smem,
            smem,
            once((128, 128), lambda i: (0, 0)),
            pl.BlockSpec((COEFFS, JOIN_BLOCKS * 128), lambda i: (0, i)),
            pl.BlockSpec(memory_space=pl.ANY),
            once((UNITS, COEFFS, 384), lambda i: (0, 0, 0)),
        ],
        out_specs=once((UNITS, COEFFS, 384), lambda i: (0, 0, 0)),
        scratch_shapes=[
            pltpu.VMEM((2 * LINES, 128), F32),
            pltpu.VMEM((DUMP + 8, 128), F32),
            pltpu.VMEM((DUMP + 8, 128), F32),
            pltpu.VMEM((128, 128), F32),
            pltpu.VMEM((256, 512), F32),
            pltpu.SemaphoreType.DMA,
        ],
        compiler_params=pltpu.CompilerParams(vmem_limit_bytes=62 << 20),
        name="join",
    )(slot, place, count, times, obs, reply, old)


PANEL = 32


def factor_kernel(gram_ref, out_ref, work_ref):
    many = gram_ref.shape[0]
    work_ref[:, 0:64, 0:128] = gram_ref[:, :, 0:128]
    work_ref[:, 0:64, 128:192] = gram_ref[:, :, 128:192]
    work_ref[:, 64:128, 64:128] = gram_ref[:, :, 192:256]
    work_ref[:, 64:128, 128:192] = gram_ref[:, :, 256:320]
    work_ref[:, 128:192, 128:192] = gram_ref[:, :, 320:384]
    work_ref[:, 64:192, 0:64] = jnp.zeros((many, 128, 64), F32)
    work_ref[:, 128:192, 64:128] = jnp.zeros((many, 64, 64), F32)
    row = lax.broadcasted_iota(I32, (many, PANEL, 192), 1)
    col = lax.broadcasted_iota(I32, (many, PANEL, 192), 2)
    thin = lax.broadcasted_iota(I32, (many, PANEL, 1), 1)
    for start in range(0, 192, PANEL):
        panel = work_ref[:, start : start + PANEL, :]
        for k in range(PANEL - 1):
            pivot = 1.0 / panel[:, k : k + 1, start + k : start + k + 1]
            column = panel[:, :, start + k : start + k + 1]
            factor = jnp.where(thin > k, column * pivot, 0.0)
            panel = panel - factor * panel[:, k : k + 1, :]
        diag = jnp.sum(jnp.where(col == row + start, panel, 0.0), axis=2, keepdims=True)
        panel = jnp.where(col >= row + start, panel * (1.0 / jnp.sqrt(diag)), 0.0)
        out_ref[:, start : start + PANEL, :] = panel
        after = start + PANEL
        if after < 192:
            for m in range(many):
                update = dot(panel[m], panel[m], ((0,), (0,)), lax.Precision.HIGHEST)
                work_ref[m, after:, :] = work_ref[m, after:, :] - update[after:, :]


def upper_factor(packed):
    many = packed.shape[0]
    vmem = pl.BlockSpec(memory_space=pltpu.VMEM)
    return pl.pallas_call(
        factor_kernel,
        out_shape=jax.ShapeDtypeStruct((many, 192, 192), F32),
        in_specs=[vmem],
        out_specs=vmem,
        scratch_shapes=[pltpu.VMEM((many, 192, 192), F32)],
        name="factor",
    )(packed)


def per_device(reference_spectra, observed, epoch_time, owner, source_row, unit):
    obs = observed[0].T
    times = epoch_time.reshape(128, 128)
    owners = owner.reshape(128, 128)
    rows = source_row.reshape(128, 128)
    units = unit.reshape(128, 128)
    scale = UNITS / (E_DEV * TM)
    third = SKY * STRIPE
    mine = lax.dynamic_slice_in_dim(reference_spectra.T, lax.axis_index("tm") * third, third, axis=1)
    stripes = mine.reshape(COEFFS, SKY, STRIPE).transpose(1, 0, 2)
    table = lax.all_to_all(stripes, "sky", split_axis=0, concat_axis=0, tiled=True)

    def one_round(state):
        number, _, gram = state
        requests, slot, place, count = route(number, owners, rows, units)
        asked = lax.all_to_all(requests, ("sky", "tm"), split_axis=0, concat_axis=0, tiled=True)
        more = jnp.max(asked[:, 255]) > 0
        replies = lax.all_to_all(serve(asked, table), ("sky", "tm"), split_axis=0, concat_axis=0, tiled=True)
        gram = join(slot, place, count, times, obs, replies.reshape(LINES, 128), gram, scale)
        return number + 1, more, gram

    start = (jnp.zeros((1,), I32), jnp.array(True), jnp.zeros((UNITS, COEFFS, 384), F32))
    _, _, gram = lax.while_loop(lambda state: state[1], one_round, start)
    shared = lax.psum_scatter(gram, "tm", scatter_dimension=0, tiled=True)
    return upper_factor(shared)[None]


def solution(mesh):
    placed = (
        P("sky", None),
        P("sky", "tm", None),
        P("sky", "tm"),
        P("sky", "tm", None),
        P("sky", "tm"),
        P("sky", "tm", None),
    )
    return jax.shard_map(
        per_device,
        mesh=mesh,
        in_specs=placed,
        out_specs=P("sky", "tm", None, None),
        check_vma=False,
    )
```

time: 1020 us -> 326 us (0.32)
  local copies, waits for them, and re-layouts: 420 us -> 10.9 us
  other arithmetic: 227 us -> 0.74 us
  waiting for transfers between devices: 277 us -> 118 us
  Pallas kernels: 0 us -> 147 us
  matrix products: 63.8 us -> 0 us
  blocking collectives: 0 us -> 18.1 us
    gather x3 -> x0, local copies, waits for them, and re-layouts: 311 us -> none  [the longest x2 246 us: per_device(): jnp.take(reference_spectra, lax.all_to_all(requests, 'sky', split_axis=0,...]
    pallas_call x0 -> x4, Pallas kernels: none -> 147 us  [the longest x1 75.4 us: join(): pl.pallas_call(functools.partial(join_kernel, scale), grid=(JOIN_STEPS,),...]
    all_to_all x2, waiting for transfers between devices: 233 us -> 87.4 us  [the longest x1 71.4 us: one_round(): lax.all_to_all(serve(asked, table), ('sky', 'tm'), split_axis=0, concat_a...]
    another operation x16 -> x0, other arithmetic: 113 us -> none  [the longest x10 110 us: upper_factor(): return jnp.swapaxes(jnp.linalg.cholesky(matrices), 1, 2)]
    scatter x1 -> x0, other arithmetic: 87.9 us -> none  [per_device(): jnp.zeros((UNITS * UCAP, column_count), design.dtype).at[unit_place]]
    dot_general x1 -> x0, matrix products: 63.1 us -> none  [per_device(): jnp.einsum('ucp,ucq->upq', buffer, buffer, precision=lax.Precision.HIGHEST)]
    scatter x1 -> x0, local copies, waits for them, and re-layouts: 61.2 us -> none  [per_device(): jnp.zeros((sky_count * CAP,), jnp.int32).at[placing].set(src_rows)]
    all_to_all x1, local copies, waits for them, and re-layouts: 22.9 us -> 1.04 us  [one_round(): lax.all_to_all(requests, ('sky', 'tm'), split_axis=0, concat_axis=0, tile...]
  transfers between devices with their start and end apart: 3 -> 3, of which waited for: 2 -> 3; matrix products, arithmetic and copies ran while one was open for 2% -> 1% of each run, Pallas kernels for 0% -> 0%
where the time goes in v1:
time: 326 us; the launch traced here: 323 us
  Pallas kernels  147 us (45%)
  waiting for transfers between devices  118 us (36%)
  blocking collectives  18.1 us (6%)
  between operations  13.4 us (4%)
  starting transfers between devices  13.3 us (4%)
  local copies, waits for them, and re-layouts  10.9 us (3%)
    pallas_call x1, Pallas kernels, join(): pl.pallas_call(functools.partial(join_kernel, scale), grid=(JOIN_STEPS,),...  75.4 us
    all_to_all x1, waiting for transfers between devices, one_round(): lax.all_to_all(serve(asked, table), ('sky', 'tm'), split_axis=0, concat_a...  71.4 us
    pallas_call x1, Pallas kernels, serve(): pl.pallas_call(serve_kernel, grid=(DEVS // PEERS_STEP,), out_shape=jax.Sh...  31.3 us
    reduce_scatter x1, waiting for transfers between devices, per_device(): shared = lax.psum_scatter(gram, 'tm', scatter_dimension=0, tiled=True)  31.1 us
    pallas_call x1, Pallas kernels, upper_factor(): pl.pallas_call(factor_kernel, out_shape=jax.ShapeDtypeStruct((many, 192,...  22.3 us
    pallas_call x1, Pallas kernels, route(): pl.pallas_call(route_kernel, out_shape=(jax.ShapeDtypeStruct((DEVS, 256),...  18.5 us
    all_to_all x1, blocking collectives, one_round(): lax.all_to_all(requests, ('sky', 'tm'), split_axis=0, concat_axis=0, tile...  18.1 us
    all_to_all x1, waiting for transfers between devices, per_device(): lax.all_to_all(stripes, 'sky', split_axis=0, concat_axis=0, tiled=True)  16 us
  transfers between devices with their start and end apart: 3, of which 3 were waited for; matrix products, arithmetic and copies ran while one was open for 1% of the time, Pallas kernels for 0%

profile of v1, /device:TPU:1, one launch (start us, length us, event | category | flops | bytes accessed | tf_op | source)
XLA Modules:
  0.0 323.3 jit_solution(9409587265453010806)
XLA Ops:
  6.5 1.3 constant_dynamic-slice_fusion
  7.8 0.3 copy.11
  8.2 1.6 copy.9
  9.7 0.0 copy-start.1
  9.7 0.0 copy-start.2
  9.7 0.0 copy-start.3
  9.7 0.0 copy-start.4
  9.8 7.7 %all-to-all-start.2 = ((f32[16,64,256]{2,1,0:T(8,128)}), f32[16,64,256]{2,1,0:T(8,128)S(1)}, u32[]{:S(2)}, u32[]{:S(2)}) async-start(f32[16,64,256]{2,1,0:T(8,128)} %copy.9), calls=%async_computation.2 | async-start | bytes 2097152 | tf_op jit(solution)/shard_map/all_to_all | solution.py:298
  17.5 0.0 reduce-scatter.2.cloned.1.call-start
  17.5 16.0 %all-to-all-done.2 = f32[16,64,256]{2,1,0:T(8,128)S(1)} async-done(((f32[16,64,256]{2,1,0:T(8,128)}), f32[16,64,256]{2,1,0:T(8,128)S(1)}, u32[]{:S(2)}, u32[]{:S(2)}) %all-to-all-start.2) | async-done | bytes 1048608 | tf_op jit(solution)/shard_map/all_to_all | solution.py:298
  33.5 2.0 broadcast_in_dim.6
  35.6 0.0 copy-done.1
  35.6 0.0 copy-done.2
  35.6 0.0 copy-done.3
  35.6 0.0 copy-done.4
  35.6 227.4 %while.12 = (s32[1]{0:T(128)}, pred[]{:T(512)}, f32[32,64,384]{2,1,0:T(8,128)}, s32[128,128]{1,0:T(8,128)S(1)}, s32[128,128]{1,0:T(8,128)S(1)}, /*index=5*/s32[1...) while((s32[1]{0:T(128)}, pred[]{:T(512)}, ...), condition=%wide.region_2.0_spmd, body=%wide.region_0.0_spmd.sunk | while | flops 129 | bytes 26477228 | solution.py:310
  35.6 18.5 %route.1 = (s32[128,256]{1,0:T(8,128)}, s32[128,128]{1,0:T(8,128)}, s32[128,128]{1,0:T(8,128)}, s32[32,128]{1,0:T(8,128)}) custom-call(s32[1]{0:T(128)} %get-tuple-element.155.round_ref, s32[128,128]{1,0:T(8,128)S(1)} %get-tuple-element.169.owner_ref, s32[128,128]{1,0:T(8,128)S(1)} %get-tuple-element.170.row_ref, s32[128,128]{1,0:T(8,128)S(1)} %get-tuple-element.171.unit_ref), custom_call_target="tpu_custom_call" | custom-call | tf_op jit(solution)/shard_map/while/body/route/pallas_call | solution.py:88
  54.0 1.0 copy.16
  55.1 18.1 %all_to_all.21 = s32[128,1,256]{2,1,0:T(1,128)S(1)} all-to-all(s32[128,1,256]{2,1,0:T(1,128)S(1)} %copy.16), channel_id=1, replica_groups=mesh['sky'=16,'tm'=8] {'sky','tm'}, dimensions={0} | all-to-all | bytes 262144 | tf_op jit(solution)/shard_map/while/body/all_to_all | solution.py:303
  73.2 0.7 copy.17
  73.9 31.3 %serve.1 = f32[128,96,128]{2,1,0:T(8,128)} custom-call(s32[128,256]{1,0:T(8,128)} %bitcast.25, f32[16,64,256]{2,1,0:T(8,128)S(1)} %get-tuple-element.172.tab_ref), custom_call_target="tpu_custom_call" | custom-call | tf_op jit(solution)/shard_map/while/body/serve/pallas_call | solution.py:129
  105.1 5.5 %all-to-all-start.1 = ((f32[128,96,128]{2,1,0:T(8,128)}), f32[128,96,128]{2,1,0:T(8,128)}, u32[]{:S(2)}, u32[]{:S(2)}) async-start(f32[128,96,128]{2,1,0:T(8,128)} %serve.1), calls=%async_computation.1 | async-start | bytes 12582912 | tf_op jit(solution)/shard_map/while/body/all_to_all | solution.py:305
  110.7 0.0 copy-start
  110.7 3.9 %copy.32.old_ref = f32[32,64,384]{2,1,0:T(8,128)} copy(f32[32,64,384]{2,1,0:T(8,128)} %get-tuple-element.157) | data formatting | bytes 6291456 | tf_op jit(solution)/shard_map/while
  114.6 0.0 copy-done
  114.6 0.7 slice_reduce_fusion.2
  116.0 71.4 %all-to-all-done.1 = f32[128,96,128]{2,1,0:T(8,128)} async-done(((f32[128,96,128]{2,1,0:T(8,128)}), f32[128,96,128]{2,1,0:T(8,128)}, u32[]{:S(2)}, u32[]{:S(2)}) %all-to-all-start.1) | async-done | bytes 6291488 | tf_op jit(solution)/shard_map/while/body/all_to_all | solution.py:305
  187.3 75.4 %join.1 = f32[32,64,384]{2,1,0:T(8,128)} custom-call(s32[128,128]{1,0:T(8,128)} %get-tuple-element.141.slot_ref, s32[128,128]{1,0:T(8,128)} %get-tuple-element.142.place_ref, s32[32,128]{1,0:T(8,128)} %get-tuple-element.143.count_ref, f32[128,128]{1,0:T(8,128)S(1)} %get-tuple-element.173.time_ref, f32[64,16384]{1,0:T(8,128)} %get-tuple-element.174.obs_ref, ...), custom_call_target="tpu_custom_call" | custom-call | tf_op jit(solution)/shard_map/while/body/join/pallas_call | solution.py:216
  263.0 0.0 reduce-scatter.2.cloned.1.call-update
  263.0 31.1 %reduce-scatter.2.cloned.1.call-done.gram_ref = f32[4,64,384]{2,1,0:T(8,128)} async-done(((f32[32,64,384]{2,1,0:T(8,128)}), f32[4,64,384]{2,1,0:T(8,128)}) %reduce-scatter.2.cloned.1.call-update) | async-done | bytes 393232 | tf_op jit(solution)/shard_map/reduce_scatter | solution.py:311
  294.1 22.3 %factor.1 = f32[4,192,192]{2,1,0:T(8,128)} custom-call(f32[4,64,384]{2,1,0:T(8,128)} %reduce-scatter.2.cloned.1.call-done.gram_ref), custom_call_target="tpu_custom_call" | custom-call | tf_op jit(solution)/shard_map/factor/pallas_call | solution.py:278
Async XLA Ops:
  9.7 25.8 %copy-start.1 = (f32[1,16384]{1,0:T(1,128)S(1)}, f32[1,16384]{1,0:T(1,128)}, u32[]{:S(2)}) copy-start(f32[1,16384]{1,0:T(1,128)} %param.10) | copy-start | bytes 196612
  9.7 25.8 %copy-start.2 = (s32[1,16384,1]{1,2,0:T(1,128)S(1)}, s32[1,16384,1]{1,2,0:T(1,128)}, u32[]{:S(2)}) copy-start(s32[1,16384,1]{1,2,0:T(1,128)} %param.11) | copy-start | bytes 196612
  9.7 25.8 %copy-start.3 = (s32[1,16384]{1,0:T(1,128)S(1)}, s32[1,16384]{1,0:T(1,128)}, u32[]{:S(2)}) copy-start(s32[1,16384]{1,0:T(1,128)} %param.12) | copy-start | bytes 196612
  9.7 25.8 %copy-start.4 = (s32[1,16384,1]{1,2,0:T(1,128)S(1)}, s32[1,16384,1]{1,2,0:T(1,128)}, u32[]{:S(2)}) copy-start(s32[1,16384,1]{1,2,0:T(1,128)} %param.13) | copy-start | bytes 196612
  9.8 23.8 %all-to-all-start.2 = ((f32[16,64,256]{2,1,0:T(8,128)}), f32[16,64,256]{2,1,0:T(8,128)S(1)}, u32[]{:S(2)}, u32[]{:S(2)}) async-start(f32[16,64,256]{2,1,0:T(8,128)} %copy.9), calls=%async_computation.2 | async-start | bytes 2097152 | tf_op jit(solution)/shard_map/all_to_all | solution.py:298
  17.5 276.6 %reduce-scatter.2.cloned.1.call-start = ((), (), s32[]{:S(2)}) async-start(), calls=%async_computation.4 | async-start | bytes 3538944 | tf_op jit(solution)/shard_map/reduce_scatter | solution.py:311
  105.1 82.2 %all-to-all-start.1 = ((f32[128,96,128]{2,1,0:T(8,128)}), f32[128,96,128]{2,1,0:T(8,128)}, u32[]{:S(2)}, u32[]{:S(2)}) async-start(f32[128,96,128]{2,1,0:T(8,128)} %serve.1), calls=%async_computation.1 | async-start | bytes 12582912 | tf_op jit(solution)/shard_map/while/body/all_to_all | solution.py:305
  110.7 3.9 %copy-start = (s32[128,1,256]{2,0,1:T(8,128)S(1)}, s32[128,1,256]{2,0,1:T(8,128)}, u32[]{:S(2)}) copy-start(s32[128,1,256]{2,0,1:T(8,128)} %copy.17) | copy-start | bytes 393220 | tf_op jit(solution)/shard_map/while
Sparse Core Ops, SparseCore 0:
  263.1 30.9 reduce-scatter.1

commit v2 on v1

--- a/solution.py
+++ b/solution.py
@@ -36,7 +36,7 @@
     before = ((tri_row < tri_col) | (tri_col >= BLOCK)).astype(BF16)
     peers = lax.broadcasted_iota(I32, (DEVS, BLOCK), 0)
     units = lax.broadcasted_iota(I32, (UNITS, BLOCK), 0)
-    ranks = lax.broadcasted_iota(I32, (SLOTS, BLOCK), 0)
+    ranks = lax.broadcasted_iota(I32, (256, BLOCK), 0)
     acc_ref[...] = jnp.zeros_like(acc_ref)
 
     def pair(ref, b):
@@ -62,7 +62,7 @@
         high = (local >> 6).astype(F32)
         low = (local & 63).astype(F32)
         values = jnp.concatenate([jnp.where(hot, high, 0.0), jnp.where(hot, low, 0.0)], axis=0).astype(BF16)
-        put = (ranks == rank).astype(BF16)
+        put = (ranks == jnp.where(active, rank + upper * (128 - HALF), 256)).astype(BF16)
         acc_ref[...] += dot(values, put, ((1,), (1,)))
         mine = (units == unit) & active
         unit_ahead = dot(mine.astype(BF16), before, ((1,), (0,)))
@@ -78,9 +78,10 @@
     base, unit_base = lax.fori_loop(0, E_DEV // BLOCK, step, start, unroll=4)
     count_ref[...] = unit_base.astype(I32)
     more = (jnp.max(base).astype(I32) > first + SLOTS).astype(I32)
-    req_ref[:, 0:128] = (acc_ref[0:DEVS, 0:128] * 64.0 + acc_ref[DEVS:, 0:128]).astype(I32)
-    tail = (acc_ref[0:DEVS, 128:] * 64.0 + acc_ref[DEVS:, 128:]).astype(I32)
-    req_ref[:, 128:] = jnp.concatenate([tail, jnp.zeros((DEVS, 256 - SLOTS), I32) + more], axis=1)
+    first_half = (acc_ref[0:DEVS, 0:128] * 64.0 + acc_ref[DEVS:, 0:128]).astype(I32)
+    lanes = lax.broadcasted_iota(I32, (DEVS, 128), 1)
+    req_ref[:, 0, :] = jnp.where(lanes < HALF, first_half, more)
+    req_ref[:, 1, :] = (acc_ref[0:DEVS, 128:] * 64.0 + acc_ref[DEVS:, 128:]).astype(I32)
 
 
 def route(number, owner, row, unit):
@@ -88,55 +89,116 @@
     return pl.pallas_call(
         route_kernel,
         out_shape=(
-            jax.ShapeDtypeStruct((DEVS, 256), I32),
+            jax.ShapeDtypeStruct((DEVS, 2, 128), I32),
             jax.ShapeDtypeStruct((128, 128), I32),
             jax.ShapeDtypeStruct((128, 128), I32),
             jax.ShapeDtypeStruct((UNITS, 128), I32),
         ),
         in_specs=[pl.BlockSpec(memory_space=pltpu.SMEM), vmem, vmem, vmem],
         out_specs=(vmem,) * 4,
-        scratch_shapes=[pltpu.VMEM((2 * DEVS, SLOTS), F32)],
+        scratch_shapes=[pltpu.VMEM((2 * DEVS, 256), F32)],
+        cost_estimate=pl.CostEstimate(flops=10_000_000_000, bytes_accessed=1_000_000, transcendentals=0),
         name="route",
     )(number, owner, row, unit)
 
 
-PEERS_STEP = 16
-
-
-def serve_kernel(req_ref, tab_ref, out_ref, rows_ref):
-    step = pl.program_id(0)
-
-    @pl.when(step == 0)
-    def _():
-        for region in range(SKY):
-            block = tab_ref[region]
-            rows_ref[region * STRIPE : (region + 1) * STRIPE, :] = jnp.concatenate([block, block], axis=0).T
+MESH = pl.DeviceIdType.MESH
+TURN = 37
+
+
+def exchange_kernel(req_ref, tab_ref, out_ref, asked_ref, rows_ref, index_ref, send_ref,
+                    ask_send, ask_recv, local, send_sem, recv_sem):
+    sky, tm = lax.axis_index("sky"), lax.axis_index("tm")
+    me = sky * TM + tm
+
+    def peer_of(k):
+        turn = lax.rem(k * TURN, DEVS)
+        x = lax.rem(lax.rem(sky, 4) + lax.rem(turn // 8, 4), 4)
+        y = lax.rem(sky // 4 + turn // 32, 4)
+        z = lax.rem(tm // 2 + lax.rem(turn // 2, 4), 4)
+        core = lax.rem(tm + turn, 2)
+        return y * 4 + x, z * 2 + core
+
+    barrier = pltpu.get_barrier_semaphore()
+
+    def greet(k, _):
+        pl.semaphore_signal(barrier, inc=1, device_id=peer_of(k), device_id_type=MESH)
+        return _
+
+    lax.fori_loop(1, DEVS, greet, 0)
+    pl.semaphore_wait(barrier, DEVS - 1)
+
+    def ask(k, _):
+        s, t = peer_of(k)
+        pltpu.make_async_remote_copy(
+            src_ref=req_ref.at[s * TM + t], dst_ref=asked_ref.at[me], send_sem=ask_send, recv_sem=ask_recv,
+            device_id=(s, t), device_id_type=MESH,
+        ).start()
+        return _
+
+    lax.fori_loop(1, DEVS, ask, 0)
+    pltpu.make_async_copy(req_ref.at[me], asked_ref.at[me], ask_recv).start()
+
+    for region in range(SKY):
+        block = tab_ref[region]
+        rows_ref[region * STRIPE : (region + 1) * STRIPE, :] = jnp.concatenate([block, block], axis=0).T
+
+    pltpu.make_async_copy(asked_ref, asked_ref, ask_recv).wait()
+    into = pltpu.make_async_copy(asked_ref, index_ref, local)
+    into.start()
+    into.wait()
 
     left = lax.broadcasted_iota(I32, (1, 128), 1) < COEFFS
 
-    def peer_rows(k, _):
-        peer = step * PEERS_STEP + k
+    def gather(peer):
         for j in range(HALF):
-            a = req_ref[peer, j]
-            b = req_ref[peer, j + HALF]
-            out_ref[k, j : j + 1, :] = jnp.where(left, rows_ref[pl.ds(a, 1), :], rows_ref[pl.ds(b, 1), :])
-        return _
-
-    lax.fori_loop(0, PEERS_STEP, peer_rows, 0)
-
-
-def serve(requests, table):
+            a = index_ref[peer, 0, j]
+            b = index_ref[peer, 1, j]
+            send_ref[peer, j : j + 1, :] = jnp.where(left, rows_ref[pl.ds(a, 1), :], rows_ref[pl.ds(b, 1), :])
+
+    def send(k):
+        s, t = peer_of(k)
+        pltpu.make_async_remote_copy(
+            src_ref=send_ref.at[s * TM + t], dst_ref=out_ref.at[me], send_sem=send_sem, recv_sem=recv_sem,
+            device_id=(s, t), device_id_type=MESH,
+        ).start()
+
+    def serve(k, _):
+        s, t = peer_of(k)
+        gather(s * TM + t)
+
+        @pl.when(k > 1)
+        def _():
+            send(k - 1)
+
+        return 0
+
+    lax.fori_loop(1, DEVS, serve, 0)
+    gather(me)
+    send(DEVS - 1)
+    pltpu.make_async_copy(send_ref.at[me], out_ref.at[me], recv_sem).start()
+    pltpu.make_async_copy(req_ref.at[pl.ds(0, DEVS - 1)], req_ref.at[pl.ds(0, DEVS - 1)], ask_send).wait()
+    pltpu.make_async_copy(send_ref.at[pl.ds(0, DEVS - 1)], send_ref.at[pl.ds(0, DEVS - 1)], send_sem).wait()
+    pltpu.make_async_copy(out_ref, out_ref, recv_sem).wait()
+
+
+def exchange(requests, table):
+    vmem = pl.BlockSpec(memory_space=pltpu.VMEM)
     return pl.pallas_call(
-        serve_kernel,
-        grid=(DEVS // PEERS_STEP,),
-        out_shape=jax.ShapeDtypeStruct((DEVS, HALF, 128), F32),
-        in_specs=[
-            pl.BlockSpec(memory_space=pltpu.SMEM),
-            pl.BlockSpec((SKY, COEFFS, STRIPE), lambda i: (0, 0, 0), pipeline_mode=pl.Buffered(1)),
-        ],
-        out_specs=pl.BlockSpec((PEERS_STEP, HALF, 128), lambda i: (i, 0, 0)),
-        scratch_shapes=[pltpu.VMEM((SKY * STRIPE, 128), F32)],
-        name="serve",
+        exchange_kernel,
+        out_shape=(
+            jax.ShapeDtypeStruct((DEVS, HALF, 128), F32),
+            jax.ShapeDtypeStruct((DEVS, 2, 128), I32),
+        ),
+        in_specs=[vmem, vmem],
+        out_specs=(pl.BlockSpec(memory_space=pl.ANY), vmem),
+        scratch_shapes=[
+            pltpu.VMEM((SKY * STRIPE, 128), F32),
+            pltpu.SMEM((DEVS, 2, 128), I32),
+            pltpu.VMEM((DEVS, HALF, 128), F32),
+        ] + [pltpu.SemaphoreType.DMA] * 5,
+        compiler_params=pltpu.CompilerParams(collective_id=0, has_side_effects=True),
+        name="exchange",
     )(requests, table)
 
 
@@ -298,16 +360,21 @@
     table = lax.all_to_all(stripes, "sky", split_axis=0, concat_axis=0, tiled=True)
 
     def one_round(state):
-        number, _, gram = state
-        requests, slot, place, count = route(number, owners, rows, units)
-        asked = lax.all_to_all(requests, ("sky", "tm"), split_axis=0, concat_axis=0, tiled=True)
-        more = jnp.max(asked[:, 255]) > 0
-        replies = lax.all_to_all(serve(asked, table), ("sky", "tm"), split_axis=0, concat_axis=0, tiled=True)
+        number, _, gram, (requests, slot, place, count) = state
+        replies, asked = exchange(requests, table)
+        more = jnp.max(asked[:, 0, 127]) > 0
         gram = join(slot, place, count, times, obs, replies.reshape(LINES, 128), gram, scale)
-        return number + 1, more, gram
-
-    start = (jnp.zeros((1,), I32), jnp.array(True), jnp.zeros((UNITS, COEFFS, 384), F32))
-    _, _, gram = lax.while_loop(lambda state: state[1], one_round, start)
+        number = number + 1
+        plan = lax.cond(
+            more,
+            lambda: route(number, owners, rows, units),
+            lambda: (requests, slot, place, count),
+        )
+        return number, more, gram, plan
+
+    number = jnp.zeros((1,), I32)
+    start = (number, jnp.array(True), jnp.zeros((UNITS, COEFFS, 384), F32), route(number, owners, rows, units))
+    gram = lax.while_loop(lambda state: state[1], one_round, start)[2]
     shared = lax.psum_scatter(gram, "tm", scatter_dimension=0, tiled=True)
     return upper_factor(shared)[None]
 

time: 326 us -> 293 us (0.90)
  waiting for transfers between devices: 118 us -> 37.4 us
  Pallas kernels: 147 us -> 219 us
  blocking collectives: 18.1 us -> 0 us
  starting transfers between devices: 13.3 us -> 7.61 us
    pallas_call x2, Pallas kernels: 49.7 us -> 122 us  [the longest x1 103 us: exchange(): pl.pallas_call(exchange_kernel, out_shape=(jax.ShapeDtypeStruct((DEVS, HA...]
    all_to_all x1 -> x0, waiting for transfers between devices: 71.4 us -> none  [one_round(): lax.all_to_all(serve(asked, table), ('sky', 'tm'), split_axis=0, concat_a...]
    all_to_all x1 -> x0, blocking collectives: 18.1 us -> none  [one_round(): lax.all_to_all(requests, ('sky', 'tm'), split_axis=0, concat_axis=0, tile...]
    all_to_all x1, waiting for transfers between devices: 16 us -> 0.01 us  [per_device(): lax.all_to_all(stripes, 'sky', split_axis=0, concat_axis=0, tiled=True)]
    reduce_scatter x1, waiting for transfers between devices: 31.1 us -> 37.4 us  [per_device(): shared = lax.psum_scatter(gram, 'tm', scatter_dimension=0, tiled=True)]
    all_to_all x1 -> x0, starting transfers between devices: 5.53 us -> none  [one_round(): lax.all_to_all(serve(asked, table), ('sky', 'tm'), split_axis=0, concat_a...]
  transfers between devices with their start and end apart: 3 -> 2, of which waited for: 3 -> 1; matrix products, arithmetic and copies ran while one was open for 1% -> 0% of each run, Pallas kernels for 0% -> 7%
where the time goes in v2:
time: 293 us; the launch traced here: 290 us
  Pallas kernels  219 us (75%)
  waiting for transfers between devices  37.4 us (13%)
  between operations  13.5 us (5%)
  local copies, waits for them, and re-layouts  9.76 us (3%)
  starting transfers between devices  7.61 us (3%)
    pallas_call x1, Pallas kernels, exchange(): pl.pallas_call(exchange_kernel, out_shape=(jax.ShapeDtypeStruct((DEVS, HA...  103 us
    pallas_call x1, Pallas kernels, join(): pl.pallas_call(functools.partial(join_kernel, scale), grid=(JOIN_STEPS,),...  74.4 us
    reduce_scatter x1, waiting for transfers between devices, per_device(): shared = lax.psum_scatter(gram, 'tm', scatter_dimension=0, tiled=True)  37.4 us
    pallas_call x1, Pallas kernels, upper_factor(): pl.pallas_call(factor_kernel, out_shape=jax.ShapeDtypeStruct((many, 192,...  22.3 us
    pallas_call x1, Pallas kernels, route(): pl.pallas_call(route_kernel, out_shape=(jax.ShapeDtypeStruct((DEVS, 2, 12...  19.2 us
    all_to_all x1, starting transfers between devices, per_device(): lax.all_to_all(stripes, 'sky', split_axis=0, concat_axis=0, tiled=True)  7.57 us
  transfers between devices with their start and end apart: 2, of which 1 were waited for; matrix products, arithmetic and copies ran while one was open for 0% of the time, Pallas kernels for 7%

profile of v2, /device:TPU:1, one launch (start us, length us, event | category | flops | bytes accessed | tf_op | source)
XLA Modules:
  0.0 290.0 jit_solution(17179489543605259621)
XLA Ops:
  6.5 1.3 constant_dynamic-slice_fusion
  7.8 0.0 copy-start.4
  7.8 0.0 copy-start.5
  7.9 0.0 copy-start.6
  7.9 0.3 copy.9
  8.2 1.6 copy.8
  9.8 7.6 %all-to-all-start = ((f32[16,64,256]{2,1,0:T(8,128)}), f32[16,64,256]{2,1,0:T(8,128)S(1)}, u32[]{:S(2)}, u32[]{:S(2)}) async-start(f32[16,64,256]{2,1,0:T(8,128)} %copy.8), calls=%async_computation | async-start | bytes 2097152 | tf_op jit(solution)/shard_map/all_to_all | solution.py:360
  17.4 0.0 reduce-scatter.2.cloned.1.call-start
  17.4 0.0 copy-done.4
  17.4 0.0 copy-done.5
  17.4 0.0 copy-done.6
  17.4 19.2 %route.3 = (s32[128,2,128]{2,1,0:T(2,128)S(1)}, s32[128,128]{1,0:T(8,128)S(1)}, s32[128,128]{1,0:T(8,128)S(1)}, s32[32,128]{1,0:T(8,128)S(1)}) custom-call(s32[1]{0:T(128)} %copy.42.round_ref, s32[128,128]{1,0:T(8,128)S(1)} %bitcast.21, s32[128,128]{1,0:T(8,128)S(1)} %bitcast.24, s32[128,128]{1,0:T(8,128)S(1)} %bitcast.26), custom_call_target="tpu_custom_call" | custom-call | flops 10000000000 | bytes 1000000 | tf_op jit(solution)/shard_map/route/pallas_call | solution.py:89
  36.6 0.0 copy-start.3
  36.6 0.0 all-to-all-done
  36.6 0.0 copy-start.2
  36.7 1.1 copy-done.2
  37.7 0.3 broadcast_in_dim.6
  38.1 0.0 copy-done.3
  38.1 183.8 %while.20 = (s32[1]{0:T(128)}, pred[]{:T(512)}, f32[32,64,384]{2,1,0:T(8,128)S(1)}, s32[128,2,128]{2,1,0:T(2,128)S(1)}, s32[128,128]{1,0:T(8,128)S(1)}, /*index=...) while((s32[1]{0:T(128)}, pred[]{:T(512)}, ...), condition=%wide.region_4.0_spmd, body=%wide.region_0.0_spmd.sunk | while | flops 10000000000 | bytes 19875128 | solution.py:377
  38.1 103.3 %exchange.1 = (f32[128,96,128]{2,1,0:T(8,128)}, s32[128,2,128]{2,1,0:T(2,128)}) custom-call(s32[128,2,128]{2,1,0:T(2,128)S(1)} %get-tuple-element.260.req_ref, f32[16,64,256]{2,1,0:T(8,128)} %get-tuple-element.279.tab_ref), custom_call_target="tpu_custom_call" | custom-call | tf_op jit(solution)/shard_map/while/body/exchange/pallas_call | solution.py:187
  141.4 1.8 slice_reduce_fusion.2
  143.8 1.6 copy.44.old_ref
  145.5 74.4 %join.1 = f32[32,64,384]{2,1,0:T(8,128)} custom-call(s32[128,128]{1,0:T(8,128)S(1)} %get-tuple-element.261.slot_ref, s32[128,128]{1,0:T(8,128)S(1)} %get-tuple-element.262.place_ref, s32[32,128]{1,0:T(8,128)S(1)} %get-tuple-element.263.count_ref, f32[128,128]{1,0:T(8,128)S(1)} %get-tuple-element.280.time_ref, f32[64,16384]{1,0:T(8,128)} %get-tuple-element.281.obs_ref, ...), custom_call_target="tpu_custom_call" | custom-call | tf_op jit(solution)/shard_map/while/body/join/pallas_call | solution.py:278
  219.9 0.0 copy-start
  220.0 1.9 copy-done
  221.8 0.0 copy-start.1
  221.8 1.6 copy-done.1
  223.5 0.0 reduce-scatter.2.cloned.1.call-update
  223.5 37.4 %reduce-scatter.2.cloned.1.call-done.gram_ref = f32[4,64,384]{2,1,0:T(8,128)} async-done(((f32[32,64,384]{2,1,0:T(8,128)}), f32[4,64,384]{2,1,0:T(8,128)}) %reduce-scatter.2.cloned.1.call-update) | async-done | bytes 393232 | tf_op jit(solution)/shard_map/reduce_scatter | solution.py:378
  260.9 22.3 %factor.1 = f32[4,192,192]{2,1,0:T(8,128)} custom-call(f32[4,64,384]{2,1,0:T(8,128)} %reduce-scatter.2.cloned.1.call-done.gram_ref), custom_call_target="tpu_custom_call" | custom-call | tf_op jit(solution)/shard_map/factor/pallas_call | solution.py:340
  (1 shorter events, 0.0 us)
Async XLA Ops:
  7.8 9.6 %copy-start.4 = (s32[1,16384,1]{1,2,0:T(1,128)S(1)}, s32[1,16384,1]{1,2,0:T(1,128)}, u32[]{:S(2)}) copy-start(s32[1,16384,1]{1,2,0:T(1,128)} %param.13) | copy-start | bytes 196612
  7.8 9.6 %copy-start.5 = (s32[1,16384]{1,0:T(1,128)S(1)}, s32[1,16384]{1,0:T(1,128)}, u32[]{:S(2)}) copy-start(s32[1,16384]{1,0:T(1,128)} %param.14) | copy-start | bytes 196612
  7.9 9.6 %copy-start.6 = (s32[1,16384,1]{1,2,0:T(1,128)S(1)}, s32[1,16384,1]{1,2,0:T(1,128)}, u32[]{:S(2)}) copy-start(s32[1,16384,1]{1,2,0:T(1,128)} %param.15) | copy-start | bytes 196612
  9.8 26.9 %all-to-all-start = ((f32[16,64,256]{2,1,0:T(8,128)}), f32[16,64,256]{2,1,0:T(8,128)S(1)}, u32[]{:S(2)}, u32[]{:S(2)}) async-start(f32[16,64,256]{2,1,0:T(8,128)} %copy.8), calls=%async_computation | async-start | bytes 2097152 | tf_op jit(solution)/shard_map/all_to_all | solution.py:360
  17.4 243.5 %reduce-scatter.2.cloned.1.call-start = ((), (), s32[]{:S(2)}) async-start(), calls=%async_computation.2 | async-start | bytes 3538944 | tf_op jit(solution)/shard_map/reduce_scatter | solution.py:378
  36.6 1.4 copy-start.3
  36.6 1.1 copy-start.2
  219.9 1.9 copy-start
  221.8 1.6 copy-start.1
Sparse Core Ops, SparseCore 0:
  223.6 37.2 reduce-scatter.1

commit v3 on v2

--- a/solution.py
+++ b/solution.py
@@ -303,48 +303,122 @@
 
 
 PANEL = 32
-
-
-def factor_kernel(gram_ref, out_ref, work_ref):
-    many = gram_ref.shape[0]
-    work_ref[:, 0:64, 0:128] = gram_ref[:, :, 0:128]
-    work_ref[:, 0:64, 128:192] = gram_ref[:, :, 128:192]
-    work_ref[:, 64:128, 64:128] = gram_ref[:, :, 192:256]
-    work_ref[:, 64:128, 128:192] = gram_ref[:, :, 256:320]
-    work_ref[:, 128:192, 128:192] = gram_ref[:, :, 320:384]
-    work_ref[:, 64:192, 0:64] = jnp.zeros((many, 128, 64), F32)
-    work_ref[:, 128:192, 64:128] = jnp.zeros((many, 64, 64), F32)
-    row = lax.broadcasted_iota(I32, (many, PANEL, 192), 1)
-    col = lax.broadcasted_iota(I32, (many, PANEL, 192), 2)
-    thin = lax.broadcasted_iota(I32, (many, PANEL, 1), 1)
-    for start in range(0, 192, PANEL):
-        panel = work_ref[:, start : start + PANEL, :]
+QUAD = UNITS // TM
+
+
+def factor(gram, out_ref, work_ref):
+    work_ref[...] = jnp.zeros_like(work_ref)
+    work_ref[:, 0:64, 0:192] = gram[:, :, 0:192]
+    work_ref[:, 64:128, 64:192] = gram[:, :, 192:320]
+    work_ref[:, 128:192, 128:192] = gram[:, :, 320:384]
+    row = lax.broadcasted_iota(I32, (PANEL, 256), 0)
+    col = lax.broadcasted_iota(I32, (PANEL, 256), 1)
+    thin = lax.broadcasted_iota(I32, (PANEL, 1), 0)
+
+    def step(i, _):
+        at = pl.multiple_of(i * PANEL, PANEL)
+        panels = [pltpu.roll(work_ref[m, pl.ds(at, PANEL), :], 256 - at, 1) for m in range(QUAD)]
         for k in range(PANEL - 1):
-            pivot = 1.0 / panel[:, k : k + 1, start + k : start + k + 1]
-            column = panel[:, :, start + k : start + k + 1]
-            factor = jnp.where(thin > k, column * pivot, 0.0)
-            panel = panel - factor * panel[:, k : k + 1, :]
-        diag = jnp.sum(jnp.where(col == row + start, panel, 0.0), axis=2, keepdims=True)
-        panel = jnp.where(col >= row + start, panel * (1.0 / jnp.sqrt(diag)), 0.0)
-        out_ref[:, start : start + PANEL, :] = panel
-        after = start + PANEL
-        if after < 192:
-            for m in range(many):
-                update = dot(panel[m], panel[m], ((0,), (0,)), lax.Precision.HIGHEST)
-                work_ref[m, after:, :] = work_ref[m, after:, :] - update[after:, :]
-
-
-def upper_factor(packed):
-    many = packed.shape[0]
+            for m in range(QUAD):
+                panel = panels[m]
+                pivot = 1.0 / panel[k : k + 1, k : k + 1]
+                below = jnp.where(thin > k, panel[:, k : k + 1] * pivot, 0.0)
+                panels[m] = panel - below * panel[k : k + 1, :]
+        for m in range(QUAD):
+            panel = panels[m]
+            diag = jnp.sum(jnp.where(col == row, panel, 0.0), axis=1, keepdims=True)
+            panel = jnp.where((col >= row) & (col < 192 - at), panel * (1.0 / jnp.sqrt(diag)), 0.0)
+            panel = pltpu.roll(panel, at, 1)
+            out_ref[m, pl.ds(at, PANEL), :] = panel[:, :192]
+            update = dot(panel, panel, ((0,), (0,)), lax.Precision.HIGHEST)
+            work_ref[m] = work_ref[m] - update[:192, :]
+        return _
+
+    lax.fori_loop(0, 192 // PANEL, step, 0)
+
+
+def reduce_kernel(gram_ref, out_ref, pair_ref, sum_ref, part_ref, relay_ref, work_ref,
+                  pair_send, pair_recv, ring_send, ring_recv):
+    sky, tm = lax.axis_index("sky"), lax.axis_index("tm")
+    z, core = tm // 2, lax.rem(tm, 2)
+    up, down, far = lax.rem(z + 1, 4), lax.rem(z + 3, 4), lax.rem(z + 2, 4)
+    partner = (sky, z * 2 + 1 - core)
+    above, below = (sky, up * 2 + core), (sky, down * 2 + core)
+
+    barrier = pltpu.get_barrier_semaphore()
+    for other in (partner, above, below):
+        pl.semaphore_signal(barrier, inc=1, device_id=other, device_id_type=MESH)
+    pl.semaphore_wait(barrier, 3)
+
+    pairs = []
+    for n, at in enumerate((far, up, down, z)):
+        copy = pltpu.make_async_remote_copy(
+            src_ref=gram_ref.at[at * 2 + 1 - core], dst_ref=pair_ref.at[at],
+            send_sem=pair_send.at[n], recv_sem=pair_recv.at[n], device_id=partner, device_id_type=MESH,
+        )
+        copy.start()
+        pairs.append(copy)
+
+    def join_pair(n, at):
+        pairs[n].wait_recv()
+        sum_ref[at] = gram_ref[at * 2 + core] + pair_ref[at]
+
+    def ring(n, src, to):
+        copy = pltpu.make_async_remote_copy(
+            src_ref=src, dst_ref=part_ref.at[n],
+            send_sem=ring_send.at[n], recv_sem=ring_recv.at[n], device_id=to, device_id_type=MESH,
+        )
+        copy.start()
+        return copy
+
+    first, second = pl.ds(0, 2), pl.ds(2, 2)
+    join_pair(0, far)
+    far_up = ring(0, sum_ref.at[far, first], above)
+    far_down = ring(1, sum_ref.at[far, second], below)
+    join_pair(1, up)
+    near_up = ring(2, sum_ref.at[up, second], above)
+    join_pair(2, down)
+    near_down = ring(3, sum_ref.at[down, first], below)
+    far_up.wait_recv()
+    relay_ref[0] = part_ref[0] + sum_ref[up, 0:2]
+    last_up = ring(4, relay_ref.at[0], above)
+    far_down.wait_recv()
+    relay_ref[1] = part_ref[1] + sum_ref[down, 2:4]
+    last_down = ring(5, relay_ref.at[1], below)
+    join_pair(3, z)
+    near_down.wait_recv()
+    near_up.wait_recv()
+    sum_ref[z, 0:2] = sum_ref[z, 0:2] + part_ref[3]
+    sum_ref[z, 2:4] = sum_ref[z, 2:4] + part_ref[2]
+    last_up.wait_recv()
+    last_down.wait_recv()
+    total = jnp.concatenate([sum_ref[z, 0:2] + part_ref[4], sum_ref[z, 2:4] + part_ref[5]], axis=0)
+    for copy in (*pairs, far_up, far_down, near_up, near_down, last_up, last_down):
+        copy.wait_send()
+    factor(total, out_ref, work_ref)
+
+
+def reduce_factor(gram):
     vmem = pl.BlockSpec(memory_space=pltpu.VMEM)
     return pl.pallas_call(
-        factor_kernel,
-        out_shape=jax.ShapeDtypeStruct((many, 192, 192), F32),
+        reduce_kernel,
+        out_shape=jax.ShapeDtypeStruct((QUAD, 192, 192), F32),
         in_specs=[vmem],
         out_specs=vmem,
-        scratch_shapes=[pltpu.VMEM((many, 192, 192), F32)],
-        name="factor",
-    )(packed)
+        scratch_shapes=[
+            pltpu.VMEM((4, QUAD, COEFFS, 384), F32),
+            pltpu.VMEM((4, QUAD, COEFFS, 384), F32),
+            pltpu.VMEM((6, 2, COEFFS, 384), F32),
+            pltpu.VMEM((2, 2, COEFFS, 384), F32),
+            pltpu.VMEM((QUAD, 192, 256), F32),
+            pltpu.SemaphoreType.DMA((4,)),
+            pltpu.SemaphoreType.DMA((4,)),
+            pltpu.SemaphoreType.DMA((6,)),
+            pltpu.SemaphoreType.DMA((6,)),
+        ],
+        compiler_params=pltpu.CompilerParams(collective_id=1, has_side_effects=True),
+        name="reduce_factor",
+    )(gram.reshape(TM, QUAD, COEFFS, 384))
 
 
 def per_device(reference_spectra, observed, epoch_time, owner, source_row, unit):
@@ -375,8 +449,7 @@
     number = jnp.zeros((1,), I32)
     start = (number, jnp.array(True), jnp.zeros((UNITS, COEFFS, 384), F32), route(number, owners, rows, units))
     gram = lax.while_loop(lambda state: state[1], one_round, start)[2]
-    shared = lax.psum_scatter(gram, "tm", scatter_dimension=0, tiled=True)
-    return upper_factor(shared)[None]
+    return reduce_factor(gram)[None]
 
 
 def solution(mesh):

time: 293 us -> 266 us (0.908)
  waiting for transfers between devices: 37.4 us -> 0.01 us
  Pallas kernels: 219 us -> 244 us
  between operations: 13.5 us -> 0.13 us
    reduce_scatter x1 -> x0, waiting for transfers between devices: 37.4 us -> none  [per_device(): shared = lax.psum_scatter(gram, 'tm', scatter_dimension=0, tiled=True)]
    pallas_call x1, Pallas kernels: 22.3 us -> 47.6 us  [reduce_factor(): pl.pallas_call(reduce_kernel, out_shape=jax.ShapeDtypeStruct((QUAD, 192,...]
  transfers between devices with their start and end apart: 2 -> 1, of which waited for: 1 -> 0; matrix products, arithmetic and copies ran while one was open for 0% -> 0% of each run, Pallas kernels for 7% -> 7%
where the time goes in v3:
time: 266 us; the launch traced here: 264 us
  Pallas kernels  244 us (92%)
  local copies, waits for them, and re-layouts  10.2 us (4%)
  starting transfers between devices  7.57 us (3%)
    pallas_call x1, Pallas kernels, exchange(): pl.pallas_call(exchange_kernel, out_shape=(jax.ShapeDtypeStruct((DEVS, HA...  103 us
    pallas_call x1, Pallas kernels, join(): pl.pallas_call(functools.partial(join_kernel, scale), grid=(JOIN_STEPS,),...  73.7 us
    pallas_call x1, Pallas kernels, reduce_factor(): pl.pallas_call(reduce_kernel, out_shape=jax.ShapeDtypeStruct((QUAD, 192,...  47.6 us
    pallas_call x1, Pallas kernels, route(): pl.pallas_call(route_kernel, out_shape=(jax.ShapeDtypeStruct((DEVS, 2, 12...  19.2 us
    all_to_all x1, starting transfers between devices, per_device(): lax.all_to_all(stripes, 'sky', split_axis=0, concat_axis=0, tiled=True)  7.57 us
  transfers between devices with their start and end apart: 1, of which 0 were waited for; matrix products, arithmetic and copies ran while one was open for 0% of the time, Pallas kernels for 7%

profile of v3, /device:TPU:1, one launch (start us, length us, event | category | flops | bytes accessed | tf_op | source)
XLA Modules:
  0.0 263.9 jit_solution(15082373549509471125)
XLA Ops:
  0.0 1.3 constant_dynamic-slice_fusion
  1.3 0.0 copy-start.3
  1.3 0.0 copy-start.4
  1.3 0.0 copy-start.5
  1.3 0.3 copy.9
  1.7 1.6 copy.8
  3.2 7.6 %all-to-all-start = ((f32[16,64,256]{2,1,0:T(8,128)}), f32[16,64,256]{2,1,0:T(8,128)S(1)}, u32[]{:S(2)}, u32[]{:S(2)}) async-start(f32[16,64,256]{2,1,0:T(8,128)} %copy.8), calls=%async_computation | async-start | bytes 2097152 | tf_op jit(solution)/shard_map/all_to_all | solution.py:434
  10.8 0.0 copy-done.3
  10.8 0.0 copy-done.4
  10.8 0.0 copy-done.5
  10.9 19.2 %route.3 = (s32[128,2,128]{2,1,0:T(2,128)S(1)}, s32[128,128]{1,0:T(8,128)S(1)}, s32[128,128]{1,0:T(8,128)S(1)}, s32[32,128]{1,0:T(8,128)S(1)}) custom-call(s32[1]{0:T(128)} %copy.43.round_ref, s32[128,128]{1,0:T(8,128)S(1)} %bitcast.24, s32[128,128]{1,0:T(8,128)S(1)} %bitcast.27, s32[128,128]{1,0:T(8,128)S(1)} %bitcast.29), custom_call_target="tpu_custom_call" | custom-call | flops 10000000000 | bytes 1000000 | tf_op jit(solution)/shard_map/route/pallas_call | solution.py:89
  30.0 0.0 copy-start.2
  30.0 0.0 all-to-all-done
  30.1 0.0 copy-start.1
  30.1 1.0 copy-done.1
  31.1 0.3 broadcast_in_dim.6
  31.5 0.0 copy-done.2
  31.5 182.7 %while.20 = (s32[1]{0:T(128)}, pred[]{:T(512)}, f32[32,64,384]{2,1,0:T(8,128)S(1)}, s32[128,2,128]{2,1,0:T(2,128)S(1)}, s32[128,128]{1,0:T(8,128)S(1)}, /*index=...) while((s32[1]{0:T(128)}, pred[]{:T(512)}, ...), condition=%wide.region_4.0_spmd, body=%wide.region_0.0_spmd.sunk | while | flops 10000000000 | bytes 19875128 | solution.py:451
  31.5 103.1 %exchange.1 = (f32[128,96,128]{2,1,0:T(8,128)}, s32[128,2,128]{2,1,0:T(2,128)}) custom-call(s32[128,2,128]{2,1,0:T(2,128)S(1)} %get-tuple-element.260.req_ref, f32[16,64,256]{2,1,0:T(8,128)} %get-tuple-element.279.tab_ref), custom_call_target="tpu_custom_call" | custom-call | tf_op jit(solution)/shard_map/while/body/exchange/pallas_call | solution.py:187
  134.6 1.8 slice_reduce_fusion.2
  137.0 1.6 copy.45.old_ref
  138.6 73.7 %join.1 = f32[32,64,384]{2,1,0:T(8,128)} custom-call(s32[128,128]{1,0:T(8,128)S(1)} %get-tuple-element.261.slot_ref, s32[128,128]{1,0:T(8,128)S(1)} %get-tuple-element.262.place_ref, s32[32,128]{1,0:T(8,128)S(1)} %get-tuple-element.263.count_ref, f32[128,128]{1,0:T(8,128)S(1)} %get-tuple-element.280.time_ref, f32[64,16384]{1,0:T(8,128)} %get-tuple-element.281.obs_ref, ...), custom_call_target="tpu_custom_call" | custom-call | tf_op jit(solution)/shard_map/while/body/join/pallas_call | solution.py:278
  212.3 0.0 copy-start
  212.3 1.9 copy-done
  214.2 47.6 %reduce_factor.1 = f32[4,192,192]{2,1,0:T(8,128)} custom-call(f32[8,4,64,384]{3,2,1,0:T(8,128)S(1)} %bitcast.18), custom_call_target="tpu_custom_call" | custom-call | tf_op jit(solution)/shard_map/reduce_factor/pallas_call | solution.py:403
  261.8 2.1 copy.46
  (1 shorter events, 0.0 us)
Async XLA Ops:
  1.3 9.5 %copy-start.3 = (s32[1,16384,1]{1,2,0:T(1,128)S(1)}, s32[1,16384,1]{1,2,0:T(1,128)}, u32[]{:S(2)}) copy-start(s32[1,16384,1]{1,2,0:T(1,128)} %param.13) | copy-start | bytes 196612
  1.3 9.5 %copy-start.4 = (s32[1,16384]{1,0:T(1,128)S(1)}, s32[1,16384]{1,0:T(1,128)}, u32[]{:S(2)}) copy-start(s32[1,16384]{1,0:T(1,128)} %param.14) | copy-start | bytes 196612
  1.3 9.5 %copy-start.5 = (s32[1,16384,1]{1,2,0:T(1,128)S(1)}, s32[1,16384,1]{1,2,0:T(1,128)}, u32[]{:S(2)}) copy-start(s32[1,16384,1]{1,2,0:T(1,128)} %param.15) | copy-start | bytes 196612
  3.2 26.8 %all-to-all-start = ((f32[16,64,256]{2,1,0:T(8,128)}), f32[16,64,256]{2,1,0:T(8,128)S(1)}, u32[]{:S(2)}, u32[]{:S(2)}) async-start(f32[16,64,256]{2,1,0:T(8,128)} %copy.8), calls=%async_computation | async-start | bytes 2097152 | tf_op jit(solution)/shard_map/all_to_all | solution.py:434
  30.0 1.4 copy-start.2
  30.1 1.1 copy-start.1
  212.3 1.9 copy-start

commit v4 on v3

--- a/solution.py
+++ b/solution.py
@@ -14,10 +14,11 @@
 TM = 8
 DEVS = SKY * TM
 E_DEV = 16384
-STRIPE = 256
-SLOTS = 192
+STRIPE = 512
+CLASSES = DEVS // 2
+SLOTS = 352
 HALF = SLOTS // 2
-LINES = DEVS * HALF
+LINES = CLASSES * HALF
 BLOCK = 256
 DUMP = UNITS * UCAP
 F32 = jnp.float32
@@ -29,14 +30,14 @@
     return lax.dot_general(a, b, (dims, ((), ())), precision=precision, preferred_element_type=F32)
 
 
-def route_kernel(round_ref, owner_ref, row_ref, unit_ref, req_ref, slot_ref, place_ref, count_ref, acc_ref):
+def route_body(round_ref, owner_ref, row_ref, unit_ref, req_ref, slot_ref, place_ref, count_ref, acc_ref):
     first = round_ref[0] * SLOTS
     tri_row = lax.broadcasted_iota(I32, (BLOCK, BLOCK + 128), 0)
     tri_col = lax.broadcasted_iota(I32, (BLOCK, BLOCK + 128), 1)
     before = ((tri_row < tri_col) | (tri_col >= BLOCK)).astype(BF16)
-    peers = lax.broadcasted_iota(I32, (DEVS, BLOCK), 0)
+    classes = lax.broadcasted_iota(I32, (CLASSES, BLOCK), 0)
     units = lax.broadcasted_iota(I32, (UNITS, BLOCK), 0)
-    ranks = lax.broadcasted_iota(I32, (256, BLOCK), 0)
+    ranks = lax.broadcasted_iota(I32, (SLOTS, BLOCK), 0)
     acc_ref[...] = jnp.zeros_like(acc_ref)
 
     def pair(ref, b):
@@ -48,96 +49,189 @@
     def step(b, carry):
         base, unit_base = carry
         owner, row, unit = pair(owner_ref, b), pair(row_ref, b), pair(unit_ref, b)
-        stripe = row >> 8
-        peer = ((stripe & (SKY - 1)) << 3) + (stripe >> 4)
-        local = (owner << 8) + (row & (STRIPE - 1))
-        hot = peers == peer
+        group = row >> 9
+        local = (owner << 9) + (row & (STRIPE - 1))
+        hot = classes == group
         ahead = dot(hot.astype(BF16), before, ((1,), (0,)))
         rank = jnp.sum(jnp.where(hot, ahead[:, :BLOCK] + wide(base), 0.0), axis=0, keepdims=True)
         rank = rank.astype(I32) - first
         active = (rank >= 0) & (rank < SLOTS)
         upper = jnp.where(rank >= HALF, 1, 0)
-        slot = upper * LINES + peer * HALF + rank - upper * HALF
+        slot = upper * LINES + group * HALF + rank - upper * HALF
         slot = jnp.where(active, slot, 0)
         high = (local >> 6).astype(F32)
         low = (local & 63).astype(F32)
         values = jnp.concatenate([jnp.where(hot, high, 0.0), jnp.where(hot, low, 0.0)], axis=0).astype(BF16)
-        put = (ranks == jnp.where(active, rank + upper * (128 - HALF), 256)).astype(BF16)
+        put = (ranks == rank).astype(BF16)
         acc_ref[...] += dot(values, put, ((1,), (1,)))
         mine = (units == unit) & active
         unit_ahead = dot(mine.astype(BF16), before, ((1,), (0,)))
         unit_rank = jnp.sum(jnp.where(mine, unit_ahead[:, :BLOCK] + wide(unit_base), 0.0), axis=0, keepdims=True)
-        place = jnp.where(active, unit * UCAP + unit_rank.astype(I32), DUMP)
+        place = jnp.where(active, unit * UCAP + unit_rank.astype(I32), DUMP) * 2
         for half in range(2):
             lanes = slice(half * 128, half * 128 + 128)
             slot_ref[pl.ds(2 * b + half, 1), :] = slot[:, lanes]
             place_ref[pl.ds(2 * b + half, 1), :] = place[:, lanes]
         return base + ahead[:, BLOCK:], unit_base + unit_ahead[:, BLOCK:]
 
-    start = (jnp.zeros((DEVS, 128), F32), jnp.zeros((UNITS, 128), F32))
+    start = (jnp.zeros((CLASSES, 128), F32), jnp.zeros((UNITS, 128), F32))
     base, unit_base = lax.fori_loop(0, E_DEV // BLOCK, step, start, unroll=4)
     count_ref[...] = unit_base.astype(I32)
     more = (jnp.max(base).astype(I32) > first + SLOTS).astype(I32)
-    first_half = (acc_ref[0:DEVS, 0:128] * 64.0 + acc_ref[DEVS:, 0:128]).astype(I32)
-    lanes = lax.broadcasted_iota(I32, (DEVS, 128), 1)
-    req_ref[:, 0, :] = jnp.where(lanes < HALF, first_half, more)
-    req_ref[:, 1, :] = (acc_ref[0:DEVS, 128:] * 64.0 + acc_ref[DEVS:, 128:]).astype(I32)
+    wanted = (acc_ref[0:CLASSES, :] * 64.0 + acc_ref[CLASSES:, :]).astype(I32)
+    req_ref[:, 0, :] = wanted[:, 0:128]
+    req_ref[:, 1, :] = wanted[:, 128:256]
+    req_ref[:, 2, :] = jnp.concatenate([wanted[:, 256:], jnp.zeros((CLASSES, 384 - SLOTS), I32)], axis=1)
+    req_ref[:, 3, :] = jnp.zeros((CLASSES, 128), I32) + more
+
+
+PLAN = (
+    jax.ShapeDtypeStruct((CLASSES, 4, 128), I32),
+    jax.ShapeDtypeStruct((128, 128), I32),
+    jax.ShapeDtypeStruct((128, 128), I32),
+    jax.ShapeDtypeStruct((UNITS, 128), I32),
+)
+SMEM_SPEC = pl.BlockSpec(memory_space=pltpu.SMEM)
+VMEM_SPEC = pl.BlockSpec(memory_space=pltpu.VMEM)
+ANY_SPEC = pl.BlockSpec(memory_space=pl.ANY)
 
 
 def route(number, owner, row, unit):
-    vmem = pl.BlockSpec(memory_space=pltpu.VMEM)
     return pl.pallas_call(
-        route_kernel,
-        out_shape=(
-            jax.ShapeDtypeStruct((DEVS, 2, 128), I32),
-            jax.ShapeDtypeStruct((128, 128), I32),
-            jax.ShapeDtypeStruct((128, 128), I32),
-            jax.ShapeDtypeStruct((UNITS, 128), I32),
-        ),
-        in_specs=[pl.BlockSpec(memory_space=pltpu.SMEM), vmem, vmem, vmem],
-        out_specs=(vmem,) * 4,
-        scratch_shapes=[pltpu.VMEM((2 * DEVS, 256), F32)],
-        cost_estimate=pl.CostEstimate(flops=10_000_000_000, bytes_accessed=1_000_000, transcendentals=0),
+        route_body,
+        out_shape=PLAN,
+        in_specs=[SMEM_SPEC, VMEM_SPEC, VMEM_SPEC, VMEM_SPEC],
+        out_specs=(VMEM_SPEC,) * 4,
+        scratch_shapes=[pltpu.VMEM((2 * CLASSES, SLOTS), F32)],
         name="route",
     )(number, owner, row, unit)
 
 
 MESH = pl.DeviceIdType.MESH
-TURN = 37
-
-
-def exchange_kernel(req_ref, tab_ref, out_ref, asked_ref, rows_ref, index_ref, send_ref,
-                    ask_send, ask_recv, local, send_sem, recv_sem):
+TURN = 11
+
+
+def position():
     sky, tm = lax.axis_index("sky"), lax.axis_index("tm")
-    me = sky * TM + tm
-
-    def peer_of(k):
-        turn = lax.rem(k * TURN, DEVS)
-        x = lax.rem(lax.rem(sky, 4) + lax.rem(turn // 8, 4), 4)
-        y = lax.rem(sky // 4 + turn // 32, 4)
-        z = lax.rem(tm // 2 + lax.rem(turn // 2, 4), 4)
-        core = lax.rem(tm + turn, 2)
-        return y * 4 + x, z * 2 + core
+    return lax.rem(sky, 4), sky // 4, tm // 2, lax.rem(tm, 2)
+
+
+def moved(at, offset, sign=1):
+    x, y, z, core = (a + sign * o for a, o in zip(at, offset))
+    return lax.rem(x + 4, 4), lax.rem(y + 4, 4), lax.rem(z + 4, 4), lax.rem(core + 2, 2)
+
+
+def mesh_id(at):
+    x, y, z, core = at
+    return y * 4 + x, z * 2 + core
+
+
+def class_of(at):
+    x, y, z, core = at
+    turned = 2 * (z // 2)
+    return (lax.rem(z, 2) * 2 + core) * 16 + lax.rem(y + turned, 4) * 4 + lax.rem(x + turned, 4)
+
+
+def near_offset(k):
+    i = lax.rem((k // 2) * TURN, 32)
+    x, y, z = lax.rem(i, 4), lax.rem(i // 4, 4), i // 16
+    hops = (x * (4 - x) + 2) // 3 + (y * (4 - y) + 2) // 3 + z
+    odd = lax.rem(x, 2) * lax.rem(y, 2)
+    flat = jnp.where(y == 2, 1, 0)
+    tall = jnp.where(odd == 1, jnp.where(x == y, 0, 1), jnp.where(x == 2, 1, 0))
+    tie = jnp.where(z == 0, flat, tall)
+    flip = jnp.where(hops > 3, 1, jnp.where(hops == 3, tie, 0))
+    return lax.rem(x + 2 * flip, 4), lax.rem(y + 2 * flip, 4), z + 2 * flip, lax.rem(k, 2)
+
+
+def prepare_kernel(round_ref, owner_ref, row_ref, unit_ref, tab_ref,
+                   table_ref, req_ref, slot_ref, place_ref, count_ref, acc_ref, send_sem, recv_sem):
+    here = position()
+    x, y, z, core = here
+    sky = y * 4 + x
+
+    def other(k):
+        return lax.rem(x + lax.rem(k, 4), 4), lax.rem(y + k // 4, 4), z, core
+
+    def piece(at):
+        return tab_ref.at[:, pl.ds(pl.multiple_of(class_of(at) * STRIPE, STRIPE), STRIPE)]
 
     barrier = pltpu.get_barrier_semaphore()
 
     def greet(k, _):
-        pl.semaphore_signal(barrier, inc=1, device_id=peer_of(k), device_id_type=MESH)
-        return _
-
-    lax.fori_loop(1, DEVS, greet, 0)
+        pl.semaphore_signal(barrier, inc=1, device_id=mesh_id(other(k)), device_id_type=MESH)
+        return _
+
+    lax.fori_loop(1, SKY, greet, 0)
+    pl.semaphore_wait(barrier, SKY - 1)
+
+    def give(k, _):
+        at = other(lax.rem(k * 7, SKY))
+        pltpu.make_async_remote_copy(
+            src_ref=piece(at), dst_ref=table_ref.at[sky], send_sem=send_sem, recv_sem=recv_sem,
+            device_id=mesh_id(at), device_id_type=MESH,
+        ).start()
+        return _
+
+    lax.fori_loop(1, SKY, give, 0)
+    pltpu.make_async_copy(piece(here), table_ref.at[sky], recv_sem).start()
+    route_body(round_ref, owner_ref, row_ref, unit_ref, req_ref, slot_ref, place_ref, count_ref, acc_ref)
+    pltpu.make_async_copy(table_ref.at[pl.ds(0, SKY - 1)], table_ref.at[pl.ds(0, SKY - 1)], send_sem).wait()
+    pltpu.make_async_copy(table_ref, table_ref, recv_sem).wait()
+
+
+def prepare(number, owner, row, unit, spectra):
+    return pl.pallas_call(
+        prepare_kernel,
+        out_shape=(jax.ShapeDtypeStruct((SKY, COEFFS, STRIPE), F32),) + PLAN,
+        in_specs=[SMEM_SPEC, VMEM_SPEC, VMEM_SPEC, VMEM_SPEC, ANY_SPEC],
+        out_specs=(VMEM_SPEC,) * 5,
+        scratch_shapes=[pltpu.VMEM((2 * CLASSES, SLOTS), F32)] + [pltpu.SemaphoreType.DMA] * 2,
+        compiler_params=pltpu.CompilerParams(collective_id=2, has_side_effects=True),
+        name="prepare",
+    )(number, owner, row, unit, spectra)
+
+
+def exchange_kernel(req_ref, tab_ref, out_ref, more_ref, rows_ref, asked_ref, flag_ref, index_ref, send_ref,
+                    ask_send, ask_recv, flag_send, flag_recv, local, send_sem, recv_sem):
+    here = position()
+    mine = class_of(here)
+    half_turn = (2, 2, 2, 0)
+
+    barrier = pltpu.get_barrier_semaphore()
+
+    def greet(k, _):
+        pl.semaphore_signal(barrier, inc=1, device_id=mesh_id(moved(here, near_offset(k))), device_id_type=MESH)
+        return _
+
+    def greet_far(k, _):
+        at = moved(moved(here, near_offset(k)), half_turn)
+        pl.semaphore_signal(barrier, inc=1, device_id=mesh_id(at), device_id_type=MESH)
+        return _
+
+    lax.fori_loop(1, CLASSES, greet, 0)
+    lax.fori_loop(0, CLASSES, greet_far, 0)
     pl.semaphore_wait(barrier, DEVS - 1)
 
     def ask(k, _):
-        s, t = peer_of(k)
+        at = moved(here, near_offset(k))
         pltpu.make_async_remote_copy(
-            src_ref=req_ref.at[s * TM + t], dst_ref=asked_ref.at[me], send_sem=ask_send, recv_sem=ask_recv,
-            device_id=(s, t), device_id_type=MESH,
+            src_ref=req_ref.at[class_of(at)], dst_ref=asked_ref.at[k], send_sem=ask_send, recv_sem=ask_recv,
+            device_id=mesh_id(at), device_id_type=MESH,
         ).start()
         return _
 
-    lax.fori_loop(1, DEVS, ask, 0)
-    pltpu.make_async_copy(req_ref.at[me], asked_ref.at[me], ask_recv).start()
+    def tell(k, _):
+        at = moved(moved(here, near_offset(k)), half_turn)
+        pltpu.make_async_remote_copy(
+            src_ref=req_ref.at[0], dst_ref=flag_ref.at[k], send_sem=flag_send, recv_sem=flag_recv,
+            device_id=mesh_id(at), device_id_type=MESH,
+        ).start()
+        return _
+
+    lax.fori_loop(1, CLASSES, ask, 0)
+    pltpu.make_async_copy(req_ref.at[mine], asked_ref.at[0], ask_recv).start()
+    lax.fori_loop(0, CLASSES, tell, 0)
 
     for region in range(SKY):
         block = tab_ref[region]
@@ -150,22 +244,20 @@
 
     left = lax.broadcasted_iota(I32, (1, 128), 1) < COEFFS
 
-    def gather(peer):
+    def gather(k):
         for j in range(HALF):
-            a = index_ref[peer, 0, j]
-            b = index_ref[peer, 1, j]
-            send_ref[peer, j : j + 1, :] = jnp.where(left, rows_ref[pl.ds(a, 1), :], rows_ref[pl.ds(b, 1), :])
+            a = index_ref[k, j // 128, j % 128]
+            b = index_ref[k, (j + HALF) // 128, (j + HALF) % 128]
+            send_ref[k, j : j + 1, :] = jnp.where(left, rows_ref[pl.ds(a, 1), :], rows_ref[pl.ds(b, 1), :])
 
     def send(k):
-        s, t = peer_of(k)
         pltpu.make_async_remote_copy(
-            src_ref=send_ref.at[s * TM + t], dst_ref=out_ref.at[me], send_sem=send_sem, recv_sem=recv_sem,
-            device_id=(s, t), device_id_type=MESH,
+            src_ref=send_ref.at[k], dst_ref=out_ref.at[mine], send_sem=send_sem, recv_sem=recv_sem,
+            device_id=mesh_id(moved(here, near_offset(k), -1)), device_id_type=MESH,
         ).start()
 
     def serve(k, _):
-        s, t = peer_of(k)
-        gather(s * TM + t)
+        gather(k)
 
         @pl.when(k > 1)
         def _():
@@ -173,30 +265,36 @@
 
         return 0
 
-    lax.fori_loop(1, DEVS, serve, 0)
-    gather(me)
-    send(DEVS - 1)
-    pltpu.make_async_copy(send_ref.at[me], out_ref.at[me], recv_sem).start()
-    pltpu.make_async_copy(req_ref.at[pl.ds(0, DEVS - 1)], req_ref.at[pl.ds(0, DEVS - 1)], ask_send).wait()
-    pltpu.make_async_copy(send_ref.at[pl.ds(0, DEVS - 1)], send_ref.at[pl.ds(0, DEVS - 1)], send_sem).wait()
+    lax.fori_loop(1, CLASSES, serve, 0)
+    gather(0)
+    send(CLASSES - 1)
+    pltpu.make_async_copy(send_ref.at[0], out_ref.at[mine], recv_sem).start()
+    most = slice(0, CLASSES - 1)
+    pltpu.make_async_copy(asked_ref.at[most], asked_ref.at[most], ask_send).wait()
+    pltpu.make_async_copy(flag_ref, flag_ref, flag_send).wait()
+    pltpu.make_async_copy(flag_ref, flag_ref, flag_recv).wait()
+    more_ref[...] = jnp.maximum(jnp.max(asked_ref[:, 3, :], axis=0, keepdims=True),
+                                jnp.max(flag_ref[:, 3, :], axis=0, keepdims=True))
+    pltpu.make_async_copy(send_ref.at[most], send_ref.at[most], send_sem).wait()
     pltpu.make_async_copy(out_ref, out_ref, recv_sem).wait()
 
 
 def exchange(requests, table):
-    vmem = pl.BlockSpec(memory_space=pltpu.VMEM)
     return pl.pallas_call(
         exchange_kernel,
         out_shape=(
-            jax.ShapeDtypeStruct((DEVS, HALF, 128), F32),
-            jax.ShapeDtypeStruct((DEVS, 2, 128), I32),
+            jax.ShapeDtypeStruct((CLASSES, HALF, 128), F32),
+            jax.ShapeDtypeStruct((1, 128), I32),
         ),
-        in_specs=[vmem, vmem],
-        out_specs=(pl.BlockSpec(memory_space=pl.ANY), vmem),
+        in_specs=[VMEM_SPEC, VMEM_SPEC],
+        out_specs=(ANY_SPEC, VMEM_SPEC),
         scratch_shapes=[
             pltpu.VMEM((SKY * STRIPE, 128), F32),
-            pltpu.SMEM((DEVS, 2, 128), I32),
-            pltpu.VMEM((DEVS, HALF, 128), F32),
-        ] + [pltpu.SemaphoreType.DMA] * 5,
+            pltpu.VMEM((CLASSES, 4, 128), I32),
+            pltpu.VMEM((CLASSES, 4, 128), I32),
+            pltpu.SMEM((CLASSES, 4, 128), I32),
+            pltpu.VMEM((CLASSES, HALF, 128), F32),
+        ] + [pltpu.SemaphoreType.DMA] * 7,
         compiler_params=pltpu.CompilerParams(collective_id=0, has_side_effects=True),
         name="exchange",
     )(requests, table)
@@ -206,14 +304,25 @@
 JOIN_BLOCKS = 128 // JOIN_STEPS
 
 
-def join_kernel(scale, slot_ref, place_ref, count_ref, time_ref, obs_ref, reply_ref, old_ref, out_ref,
-                rows_ref, x0_ref, x1_ref, block_ref, sums_ref, sem):
+def join_kernel(scale, number_ref, slot_ref, place_ref, count_ref, time_ref, obs_ref, reply_ref, old_ref, out_ref,
+                rows_ref, x_ref, block_ref, sums_ref, sem, old_sem):
     step = pl.program_id(0)
 
     @pl.when(step == 0)
     def _():
         copy = pltpu.make_async_copy(reply_ref, rows_ref.at[pl.ds(0, LINES), :], sem)
         copy.start()
+
+        @pl.when(number_ref[0] == 0)
+        def _():
+            out_ref[...] = jnp.zeros_like(out_ref)
+
+        @pl.when(number_ref[0] > 0)
+        def _():
+            before = pltpu.make_async_copy(old_ref, out_ref, old_sem)
+            before.start()
+            before.wait()
+
         copy.wait()
 
         def turn(i, _):
@@ -229,14 +338,16 @@
         b = step * JOIN_BLOCKS + k
         at = pl.multiple_of(k * 128, 128)
         times = jnp.broadcast_to(time_ref[pl.ds(b, 1), :], (COEFFS, 128))
-        block_ref[...] = jnp.concatenate([times, obs_ref[:, pl.ds(at, 128)]], axis=0).T
+        plain = jnp.concatenate([jnp.ones((COEFFS, 128), F32), obs_ref[:, pl.ds(at, 128)]], axis=0)
+        timed = jnp.concatenate([times, jnp.zeros((COEFFS, 128), F32)], axis=0)
+        block_ref[pl.ds(0, 128, stride=2), :] = plain.T
+        block_ref[pl.ds(1, 128, stride=2), :] = timed.T
         for j in range(128):
             s = slot_ref[b, j]
             p = place_ref[b, j]
-            r = rows_ref[pl.ds(s, 1), :]
-            o = block_ref[j : j + 1, :]
-            x0_ref[pl.ds(p, 1), :] = jnp.where(left, r, o)
-            x1_ref[pl.ds(p, 1), :] = r * o
+            r = rows_ref[pl.ds(s, 2, stride=0), :]
+            o = block_ref[2 * j : 2 * j + 2, :]
+            x_ref[pl.ds(p, 2), :] = jnp.where(left, r * o, o)
         return _
 
     lax.fori_loop(0, JOIN_BLOCKS, place_block, 0)
@@ -249,7 +360,9 @@
 
             def add(i, _):
                 at = pl.multiple_of(u * UCAP + i * 256, 256)
-                x = jnp.concatenate([x0_ref[pl.ds(at, 256), :], x1_ref[pl.ds(at, 256), :]], axis=1)
+                x = jnp.concatenate(
+                    [x_ref[pl.ds(2 * at, 256, stride=2), :], x_ref[pl.ds(2 * at + 1, 256, stride=2), :]], axis=1
+                )
                 rows = lax.broadcasted_iota(I32, (256, 256), 0) + i * 256
                 x = jnp.where(rows < count, x, 0.0)
                 high = x.astype(BF16)
@@ -264,15 +377,15 @@
             ref = slice(0, 64)
             obs = slice(64, 128)
             tim = slice(128, 192)
-            out_ref[u, :, 0:128] = old_ref[u, :, 0:128] + jnp.where(left, gram[ref, 0:128], turned[ref, 128:256])
-            out_ref[u, :, 128:256] = old_ref[u, :, 128:256] + jnp.where(left, turned[ref, 128:256], turned[tim, 128:256])
-            out_ref[u, :, 256:384] = old_ref[u, :, 256:384] + jnp.where(left, turned[tim, 128:256], gram[obs, 0:128])
+            out_ref[u, :, 0:128] = out_ref[u, :, 0:128] + jnp.where(left, gram[ref, 0:128], turned[ref, 128:256])
+            out_ref[u, :, 128:256] = out_ref[u, :, 128:256] + jnp.where(left, turned[ref, 128:256], turned[tim, 128:256])
+            out_ref[u, :, 256:384] = out_ref[u, :, 256:384] + jnp.where(left, turned[tim, 128:256], gram[obs, 0:128])
             return _
 
         lax.fori_loop(0, UNITS, unit_gram, 0)
 
 
-def join(slot, place, count, times, obs, reply, old, scale):
+def join(number, slot, place, count, times, obs, reply, old, scale):
     smem = pl.BlockSpec(memory_space=pltpu.SMEM)
     once = functools.partial(pl.BlockSpec, pipeline_mode=pl.Buffered(1))
     return pl.pallas_call(
@@ -283,23 +396,24 @@
             smem,
             smem,
             smem,
+            smem,
             once((128, 128), lambda i: (0, 0)),
             pl.BlockSpec((COEFFS, JOIN_BLOCKS * 128), lambda i: (0, i)),
-            pl.BlockSpec(memory_space=pl.ANY),
-            once((UNITS, COEFFS, 384), lambda i: (0, 0, 0)),
+            ANY_SPEC,
+            ANY_SPEC,
         ],
         out_specs=once((UNITS, COEFFS, 384), lambda i: (0, 0, 0)),
         scratch_shapes=[
-            pltpu.VMEM((2 * LINES, 128), F32),
-            pltpu.VMEM((DUMP + 8, 128), F32),
-            pltpu.VMEM((DUMP + 8, 128), F32),
-            pltpu.VMEM((128, 128), F32),
+            pltpu.VMEM((2 * LINES + 8, 128), F32),
+            pltpu.VMEM((2 * DUMP + 8, 128), F32),
+            pltpu.VMEM((256, 128), F32),
             pltpu.VMEM((256, 512), F32),
+            pltpu.SemaphoreType.DMA,
             pltpu.SemaphoreType.DMA,
         ],
         compiler_params=pltpu.CompilerParams(vmem_limit_bytes=62 << 20),
         name="join",
-    )(slot, place, count, times, obs, reply, old)
+    )(number, slot, place, count, times, obs, reply, old)
 
 
 PANEL = 32
@@ -428,26 +542,20 @@
     rows = source_row.reshape(128, 128)
     units = unit.reshape(128, 128)
     scale = UNITS / (E_DEV * TM)
-    third = SKY * STRIPE
-    mine = lax.dynamic_slice_in_dim(reference_spectra.T, lax.axis_index("tm") * third, third, axis=1)
-    stripes = mine.reshape(COEFFS, SKY, STRIPE).transpose(1, 0, 2)
-    table = lax.all_to_all(stripes, "sky", split_axis=0, concat_axis=0, tiled=True)
+    number = jnp.zeros((1,), I32)
+    table, *plan = prepare(number, owners, rows, units, reference_spectra.T)
 
     def one_round(state):
-        number, _, gram, (requests, slot, place, count) = state
-        replies, asked = exchange(requests, table)
-        more = jnp.max(asked[:, 0, 127]) > 0
-        gram = join(slot, place, count, times, obs, replies.reshape(LINES, 128), gram, scale)
+        number, _, gram, plan = state
+        requests, slot, place, count = plan
+        replies, flags = exchange(requests, table)
+        more = flags[0, 0] > 0
+        gram = join(number, slot, place, count, times, obs, replies.reshape(LINES, 128), gram, scale)
         number = number + 1
-        plan = lax.cond(
-            more,
-            lambda: route(number, owners, rows, units),
-            lambda: (requests, slot, place, count),
-        )
+        plan = lax.cond(more, lambda: tuple(route(number, owners, rows, units)), lambda: plan)
         return number, more, gram, plan
 
-    number = jnp.zeros((1,), I32)
-    start = (number, jnp.array(True), jnp.zeros((UNITS, COEFFS, 384), F32), route(number, owners, rows, units))
+    start = (number, jnp.array(True), jnp.zeros((UNITS, COEFFS, 384), F32), tuple(plan))
     gram = lax.while_loop(lambda state: state[1], one_round, start)[2]
     return reduce_factor(gram)[None]
 

time: 266 us -> 258 us (0.970); the launches traced: 264 us -> 253 us
  starting transfers between devices: 7.57 us -> 0 us
    all_to_all x1 -> x0, starting transfers between devices: 7.57 us -> none  [per_device(): lax.all_to_all(stripes, 'sky', split_axis=0, concat_axis=0, tiled=True)]
    pallas_call x2, Pallas kernels: 122 us -> 125 us  [the longest x1 91.4 us: exchange(): pl.pallas_call(exchange_kernel, out_shape=(jax.ShapeDtypeStruct((CLASSES,...]
  transfers between devices with their start and end apart: 1 -> 0, of which waited for: 0 -> 0; matrix products, arithmetic and copies ran while one was open for 0% -> 0% of each run, Pallas kernels for 7% -> 0%
where the time goes in v4:
time: 258 us; the launch traced here: 253 us
  Pallas kernels  244 us (95%)
  local copies, waits for them, and re-layouts  8.04 us (3%)
    pallas_call x1, Pallas kernels, exchange(): pl.pallas_call(exchange_kernel, out_shape=(jax.ShapeDtypeStruct((CLASSES,...  91.4 us
    pallas_call x1, Pallas kernels, join(): pl.pallas_call(functools.partial(join_kernel, scale), grid=(JOIN_STEPS,),...  71.9 us
    pallas_call x1, Pallas kernels, reduce_factor(): pl.pallas_call(reduce_kernel, out_shape=jax.ShapeDtypeStruct((QUAD, 192,...  47.2 us
    pallas_call x1, Pallas kernels, prepare(): pl.pallas_call(prepare_kernel, out_shape=(jax.ShapeDtypeStruct((SKY, COEF...  33.8 us

profile of v4, /device:TPU:1, one launch (start us, length us, event | category | flops | bytes accessed | tf_op | source)
XLA Modules:
  0.0 253.0 jit_solution(12372320139134195295)
XLA Ops:
  0.0 33.8 %prepare.1 = (f32[16,64,512]{2,1,0:T(8,128)}, s32[64,4,128]{2,1,0:T(4,128)S(1)}, s32[128,128]{1,0:T(8,128)S(1)}, s32[128,128]{1,0:T(8,128)S(1)}, s32[32,128]{1,0:T(8,128)S(1)}) custom-call(s32[1]{0:T(128)} %copy.40.round_ref, s32[128,128]{1,0:T(8,128)} %bitcast.20, s32[128,128]{1,0:T(8,128)} %bitcast.22, s32[128,128]{1,0:T(8,128)} %bitcast.24, ...), custom_call_target="tpu_custom_call" | custom-call | tf_op jit(solution)/shard_map/prepare/pallas_call | solution.py:184
  33.8 0.0 copy-start
  33.8 0.0 copy-start.1
  33.9 0.0 copy-start.2
  33.9 0.0 copy-start.3
  33.9 2.0 broadcast_in_dim.6
  35.9 0.0 copy-done
  35.9 0.0 copy-done.1
  35.9 0.0 copy-done.2
  35.9 0.0 copy-done.3
  35.9 167.9 %while.20 = (s32[1]{0:T(128)}, pred[]{:T(512)}, f32[32,64,384]{2,1,0:T(8,128)}, s32[64,4,128]{2,1,0:T(4,128)S(1)}, s32[128,128]{1,0:T(8,128)S(1)}, /*index=5*/s3...) while((s32[1]{0:T(128)}, pred[]{:T(512)}, ...), condition=%wide.region_3.0_spmd, body=%wide.region_0.0_spmd | while | flops 3 | bytes 6291682 | solution.py:559
  35.9 91.4 %exchange.1 = (f32[64,176,128]{2,1,0:T(8,128)}, s32[1,128]{1,0:T(1,128)}) custom-call(s32[64,4,128]{2,1,0:T(4,128)S(1)} %get-tuple-element.231.req_ref, f32[16,64,512]{2,1,0:T(8,128)} %get-tuple-element.250.tab_ref), custom_call_target="tpu_custom_call" | custom-call | tf_op jit(solution)/shard_map/while/body/exchange/pallas_call | solution.py:283
  127.9 4.0 %copy.42.old_ref = f32[32,64,384]{2,1,0:T(8,128)} copy(f32[32,64,384]{2,1,0:T(8,128)} %get-tuple-element.230) | data formatting | bytes 6291456 | tf_op jit(solution)/shard_map/while
  131.9 71.9 %join.1 = f32[32,64,384]{2,1,0:T(8,128)} custom-call(s32[1]{0:T(128)S(6)} %copy.22.number_ref, s32[128,128]{1,0:T(8,128)S(1)} %get-tuple-element.232.slot_ref, s32[128,128]{1,0:T(8,128)S(1)} %get-tuple-element.233.place_ref, s32[32,128]{1,0:T(8,128)S(1)} %get-tuple-element.234.count_ref, f32[128,128]{1,0:T(8,128)S(1)} %get-tuple-element.251.time_ref, ...), custom_call_target="tpu_custom_call" | custom-call | tf_op jit(solution)/shard_map/while/body/join/pallas_call | solution.py:391
  203.8 47.2 %reduce_factor.1 = f32[4,192,192]{2,1,0:T(8,128)} custom-call(f32[8,4,64,384]{3,2,1,0:T(8,128)} %bitcast.9.gram_ref), custom_call_target="tpu_custom_call" | custom-call | tf_op jit(solution)/shard_map/reduce_factor/pallas_call | solution.py:517
  251.0 2.1 copy.43
  (1 shorter events, 0.0 us)
Async XLA Ops:
  33.8 2.0 copy-start
  33.8 2.0 copy-start.1
  33.9 2.0 copy-start.2
  33.9 2.0 copy-start.3

commit v5 on v4

--- a/solution.py
+++ b/solution.py
@@ -111,14 +111,27 @@
 TURN = 11
 
 
+def nearer(i):
+    x, y, z = i % 4, i // 4 % 4, i // 16
+    hops = min(x, 4 - x) + min(y, 4 - y) + z
+    if hops != 3:
+        return int(hops > 3)
+    if z == 0:
+        return int(y == 2)
+    return int(x != y) if x % 2 and y % 2 else int(x == 2)
+
+
+FLIPS = sum(nearer(i) << i for i in range(32))
+
+
 def position():
     sky, tm = lax.axis_index("sky"), lax.axis_index("tm")
-    return lax.rem(sky, 4), sky // 4, tm // 2, lax.rem(tm, 2)
-
-
-def moved(at, offset, sign=1):
-    x, y, z, core = (a + sign * o for a, o in zip(at, offset))
-    return lax.rem(x + 4, 4), lax.rem(y + 4, 4), lax.rem(z + 4, 4), lax.rem(core + 2, 2)
+    return sky & 3, sky >> 2, tm >> 1, tm & 1
+
+
+def moved(at, offset):
+    x, y, z, core = (a + o for a, o in zip(at, offset))
+    return x & 3, y & 3, z & 3, core & 1
 
 
 def mesh_id(at):
@@ -128,20 +141,19 @@
 
 def class_of(at):
     x, y, z, core = at
-    turned = 2 * (z // 2)
-    return (lax.rem(z, 2) * 2 + core) * 16 + lax.rem(y + turned, 4) * 4 + lax.rem(x + turned, 4)
+    turned = z & 2
+    return ((z & 1) * 2 + core) * 16 + ((y + turned) & 3) * 4 + ((x + turned) & 3)
 
 
 def near_offset(k):
-    i = lax.rem((k // 2) * TURN, 32)
-    x, y, z = lax.rem(i, 4), lax.rem(i // 4, 4), i // 16
-    hops = (x * (4 - x) + 2) // 3 + (y * (4 - y) + 2) // 3 + z
-    odd = lax.rem(x, 2) * lax.rem(y, 2)
-    flat = jnp.where(y == 2, 1, 0)
-    tall = jnp.where(odd == 1, jnp.where(x == y, 0, 1), jnp.where(x == 2, 1, 0))
-    tie = jnp.where(z == 0, flat, tall)
-    flip = jnp.where(hops > 3, 1, jnp.where(hops == 3, tie, 0))
-    return lax.rem(x + 2 * flip, 4), lax.rem(y + 2 * flip, 4), z + 2 * flip, lax.rem(k, 2)
+    i = ((k >> 1) * TURN) & 31
+    flip = ((FLIPS >> i) & 1) * 2
+    return (i & 3) + flip, (i >> 2) + flip, (i >> 4) + flip, k & 1
+
+
+def next_device(k):
+    to = lax.axis_index("sky") * TM + lax.axis_index("tm") + k
+    return (to >> 3) & (SKY - 1), to & (TM - 1)
 
 
 def prepare_kernel(round_ref, owner_ref, row_ref, unit_ref, tab_ref,
@@ -151,7 +163,7 @@
     sky = y * 4 + x
 
     def other(k):
-        return lax.rem(x + lax.rem(k, 4), 4), lax.rem(y + k // 4, 4), z, core
+        return (x + k) & 3, (y + (k >> 2)) & 3, z, core
 
     def piece(at):
         return tab_ref.at[:, pl.ds(pl.multiple_of(class_of(at) * STRIPE, STRIPE), STRIPE)]
@@ -166,7 +178,7 @@
     pl.semaphore_wait(barrier, SKY - 1)
 
     def give(k, _):
-        at = other(lax.rem(k * 7, SKY))
+        at = other((k * 7) & (SKY - 1))
         pltpu.make_async_remote_copy(
             src_ref=piece(at), dst_ref=table_ref.at[sky], send_sem=send_sem, recv_sem=recv_sem,
             device_id=mesh_id(at), device_id_type=MESH,
@@ -201,16 +213,10 @@
     barrier = pltpu.get_barrier_semaphore()
 
     def greet(k, _):
-        pl.semaphore_signal(barrier, inc=1, device_id=mesh_id(moved(here, near_offset(k))), device_id_type=MESH)
-        return _
-
-    def greet_far(k, _):
-        at = moved(moved(here, near_offset(k)), half_turn)
-        pl.semaphore_signal(barrier, inc=1, device_id=mesh_id(at), device_id_type=MESH)
-        return _
-
-    lax.fori_loop(1, CLASSES, greet, 0)
-    lax.fori_loop(0, CLASSES, greet_far, 0)
+        pl.semaphore_signal(barrier, inc=1, device_id=next_device(k), device_id_type=MESH)
+        return _
+
+    lax.fori_loop(1, DEVS, greet, 0)
     pl.semaphore_wait(barrier, DEVS - 1)
 
     def ask(k, _):
@@ -253,7 +259,7 @@
     def send(k):
         pltpu.make_async_remote_copy(
             src_ref=send_ref.at[k], dst_ref=out_ref.at[mine], send_sem=send_sem, recv_sem=recv_sem,
-            device_id=mesh_id(moved(here, near_offset(k), -1)), device_id_type=MESH,
+            device_id=mesh_id(moved(here, [-o for o in near_offset(k)])), device_id_type=MESH,
         ).start()
 
     def serve(k, _):
@@ -279,7 +285,7 @@
     pltpu.make_async_copy(out_ref, out_ref, recv_sem).wait()
 
 
-def exchange(requests, table):
+def exchange(collective, requests, table):
     return pl.pallas_call(
         exchange_kernel,
         out_shape=(
@@ -295,7 +301,7 @@
             pltpu.SMEM((CLASSES, 4, 128), I32),
             pltpu.VMEM((CLASSES, HALF, 128), F32),
         ] + [pltpu.SemaphoreType.DMA] * 7,
-        compiler_params=pltpu.CompilerParams(collective_id=0, has_side_effects=True),
+        compiler_params=pltpu.CompilerParams(collective_id=collective, has_side_effects=True),
         name="exchange",
     )(requests, table)
 
@@ -304,8 +310,8 @@
 JOIN_BLOCKS = 128 // JOIN_STEPS
 
 
-def join_kernel(scale, number_ref, slot_ref, place_ref, count_ref, time_ref, obs_ref, reply_ref, old_ref, out_ref,
-                rows_ref, x_ref, block_ref, sums_ref, sem, old_sem):
+def join_kernel(scale, slot_ref, place_ref, count_ref, time_ref, obs_ref, reply_ref, *refs):
+    *old_ref, out_ref, rows_ref, x_ref, block_ref, sums_ref, sem, old_sem = refs
     step = pl.program_id(0)
 
     @pl.when(step == 0)
@@ -313,16 +319,10 @@
         copy = pltpu.make_async_copy(reply_ref, rows_ref.at[pl.ds(0, LINES), :], sem)
         copy.start()
 
-        @pl.when(number_ref[0] == 0)
-        def _():
-            out_ref[...] = jnp.zeros_like(out_ref)
-
-        @pl.when(number_ref[0] > 0)
-        def _():
-            before = pltpu.make_async_copy(old_ref, out_ref, old_sem)
+        for old in old_ref:
+            before = pltpu.make_async_copy(old, out_ref, old_sem)
             before.start()
             before.wait()
-
         copy.wait()
 
         def turn(i, _):
@@ -354,6 +354,10 @@
 
     @pl.when(step == JOIN_STEPS - 1)
     def _():
+        def put(u, at, value):
+            lanes = slice(at, at + 128)
+            out_ref[u, :, lanes] = out_ref[u, :, lanes] + value if old_ref else value
+
         def unit_gram(u, _):
             count = count_ref[u, 0]
             sums_ref[...] = jnp.zeros_like(sums_ref)
@@ -377,15 +381,15 @@
             ref = slice(0, 64)
             obs = slice(64, 128)
             tim = slice(128, 192)
-            out_ref[u, :, 0:128] = out_ref[u, :, 0:128] + jnp.where(left, gram[ref, 0:128], turned[ref, 128:256])
-            out_ref[u, :, 128:256] = out_ref[u, :, 128:256] + jnp.where(left, turned[ref, 128:256], turned[tim, 128:256])
-            out_ref[u, :, 256:384] = out_ref[u, :, 256:384] + jnp.where(left, turned[tim, 128:256], gram[obs, 0:128])
+            put(u, 0, jnp.where(left, gram[ref, 0:128], turned[ref, 128:256]))
+            put(u, 128, jnp.where(left, turned[ref, 128:256], turned[tim, 128:256]))
+            put(u, 256, jnp.where(left, turned[tim, 128:256], gram[obs, 0:128]))
             return _
 
         lax.fori_loop(0, UNITS, unit_gram, 0)
 
 
-def join(number, slot, place, count, times, obs, reply, old, scale):
+def join(plan, times, obs, reply, scale, *old):
     smem = pl.BlockSpec(memory_space=pltpu.SMEM)
     once = functools.partial(pl.BlockSpec, pipeline_mode=pl.Buffered(1))
     return pl.pallas_call(
@@ -396,12 +400,10 @@
             smem,
             smem,
             smem,
-            smem,
             once((128, 128), lambda i: (0, 0)),
             pl.BlockSpec((COEFFS, JOIN_BLOCKS * 128), lambda i: (0, i)),
             ANY_SPEC,
-            ANY_SPEC,
-        ],
+        ] + [ANY_SPEC] * len(old),
         out_specs=once((UNITS, COEFFS, 384), lambda i: (0, 0, 0)),
         scratch_shapes=[
             pltpu.VMEM((2 * LINES + 8, 128), F32),
@@ -413,11 +415,21 @@
         ],
         compiler_params=pltpu.CompilerParams(vmem_limit_bytes=62 << 20),
         name="join",
-    )(number, slot, place, count, times, obs, reply, old)
+    )(*plan[1:], times, obs, reply.reshape(LINES, 128), *old)
 
 
 PANEL = 32
 QUAD = UNITS // TM
+
+
+def square(x):
+    high = x.astype(BF16)
+    rest = x - high.astype(F32)
+    mid = rest.astype(BF16)
+    low = (rest - mid.astype(F32)).astype(BF16)
+    one = jnp.concatenate([high, high, mid, high, low, mid], axis=0)
+    two = jnp.concatenate([high, mid, high, low, high, mid], axis=0)
+    return dot(one, two, ((0,), (0,)))
 
 
 def factor(gram, out_ref, work_ref):
@@ -432,19 +444,29 @@
     def step(i, _):
         at = pl.multiple_of(i * PANEL, PANEL)
         panels = [pltpu.roll(work_ref[m, pl.ds(at, PANEL), :], 256 - at, 1) for m in range(QUAD)]
-        for k in range(PANEL - 1):
+        for k in range(0, PANEL - 2, 2):
             for m in range(QUAD):
                 panel = panels[m]
-                pivot = 1.0 / panel[k : k + 1, k : k + 1]
-                below = jnp.where(thin > k, panel[:, k : k + 1] * pivot, 0.0)
-                panels[m] = panel - below * panel[k : k + 1, :]
+                p, q = panel[k : k + 1, :], panel[k + 1 : k + 2, :]
+                a, b, c = p[:, k : k + 1], p[:, k + 1 : k + 2], q[:, k + 1 : k + 2]
+                inverse = 1.0 / (a * c - b * b)
+                u = (c * inverse) * p - (b * inverse) * q
+                v = (a * inverse) * q - (b * inverse) * p
+                left = jnp.where(thin > k + 1, panel[:, k : k + 1], 0.0)
+                right = jnp.where(thin > k + 1, panel[:, k + 1 : k + 2], 0.0)
+                panels[m] = panel - left * u - right * v
         for m in range(QUAD):
             panel = panels[m]
+            above = pltpu.roll(panel, 1, 0)
+            b = jnp.sum(jnp.where(col == row, above, 0.0), axis=1, keepdims=True)
+            a = jnp.sum(jnp.where(col == row - 1, above, 0.0), axis=1, keepdims=True)
+            second = (thin & 1) == 1
+            panel = panel - jnp.where(second, b / jnp.where(second, a, 1.0), 0.0) * above
             diag = jnp.sum(jnp.where(col == row, panel, 0.0), axis=1, keepdims=True)
             panel = jnp.where((col >= row) & (col < 192 - at), panel * (1.0 / jnp.sqrt(diag)), 0.0)
             panel = pltpu.roll(panel, at, 1)
             out_ref[m, pl.ds(at, PANEL), :] = panel[:, :192]
-            update = dot(panel, panel, ((0,), (0,)), lax.Precision.HIGHEST)
+            update = square(panel)
             work_ref[m] = work_ref[m] - update[:192, :]
         return _
 
@@ -545,18 +567,17 @@
     number = jnp.zeros((1,), I32)
     table, *plan = prepare(number, owners, rows, units, reference_spectra.T)
 
-    def one_round(state):
-        number, _, gram, plan = state
-        requests, slot, place, count = plan
-        replies, flags = exchange(requests, table)
-        more = flags[0, 0] > 0
-        gram = join(number, slot, place, count, times, obs, replies.reshape(LINES, 128), gram, scale)
+    replies, more = exchange(0, plan[0], table)
+    gram = join(plan, times, obs, replies, scale)
+
+    def next_round(state):
+        number, _, gram = state
         number = number + 1
-        plan = lax.cond(more, lambda: tuple(route(number, owners, rows, units)), lambda: plan)
-        return number, more, gram, plan
-
-    start = (number, jnp.array(True), jnp.zeros((UNITS, COEFFS, 384), F32), tuple(plan))
-    gram = lax.while_loop(lambda state: state[1], one_round, start)[2]
+        plan = route(number, owners, rows, units)
+        replies, more = exchange(3, plan[0], table)
+        return number, more, join(plan, times, obs, replies, scale, gram)
+
+    gram = lax.while_loop(lambda state: state[1][0, 0] > 0, next_round, (number, more, gram))[2]
     return reduce_factor(gram)[None]
 
 

time: 258 us -> 243 us (0.942)
  Pallas kernels: 244 us -> 236 us
  local copies, waits for them, and re-layouts: 8.04 us -> 3.44 us
    pallas_call x1, Pallas kernels: 91.4 us -> 82.5 us  [exchange(): pl.pallas_call(exchange_kernel, out_shape=(jax.ShapeDtypeStruct((CLASSES,...]
    while x1 -> x0, local copies, waits for them, and re-layouts: 3.96 us -> none
where the time goes in v5:
time: 243 us; the launch traced here: 240 us
  Pallas kernels  236 us (97%)
  local copies, waits for them, and re-layouts  3.44 us (1%)
    pallas_call x1, Pallas kernels, exchange(): pl.pallas_call(exchange_kernel, out_shape=(jax.ShapeDtypeStruct((CLASSES,...  82.5 us
    pallas_call x1, Pallas kernels, join(): pl.pallas_call(functools.partial(join_kernel, scale), grid=(JOIN_STEPS,),...  72.6 us
    pallas_call x1, Pallas kernels, reduce_factor(): pl.pallas_call(reduce_kernel, out_shape=jax.ShapeDtypeStruct((QUAD, 192,...  47.8 us
    pallas_call x1, Pallas kernels, prepare(): pl.pallas_call(prepare_kernel, out_shape=(jax.ShapeDtypeStruct((SKY, COEF...  33.2 us

profile of v5, /device:TPU:1, one launch (start us, length us, event | category | flops | bytes accessed | tf_op | source)
XLA Modules:
  0.0 240.3 jit_solution(6392269873333384778)
XLA Ops:
  0.0 0.0 copy-start.2
  0.0 33.2 %prepare.1 = (f32[16,64,512]{2,1,0:T(8,128)S(1)}, s32[64,4,128]{2,1,0:T(4,128)}, s32[128,128]{1,0:T(8,128)}, s32[128,128]{1,0:T(8,128)}, s32[32,128]{1,0:T(8,128)}) custom-call(s32[1]{0:T(128)} %copy.19.round_ref, s32[128,128]{1,0:T(8,128)} %bitcast.26, s32[128,128]{1,0:T(8,128)} %bitcast.28, s32[128,128]{1,0:T(8,128)} %bitcast.30, f32[64,32768]{1,0:T(8,128)} %bitcast.21), custom_call_target="tpu_custom_call" | custom-call | tf_op jit(solution)/shard_map/prepare/pallas_call | solution.py:196
  33.2 0.0 copy-start
  33.2 1.3 copy-done
  34.6 82.5 %exchange.2 = (f32[64,176,128]{2,1,0:T(8,128)}, s32[1,128]{1,0:T(1,128)}) custom-call(s32[64,4,128]{2,1,0:T(4,128)} %get-tuple-element.64.req_ref, f32[16,64,512]{2,1,0:T(8,128)S(1)} %get-tuple-element.147.tab_ref), custom_call_target="tpu_custom_call" | custom-call | tf_op jit(solution)/shard_map/exchange/pallas_call | solution.py:289
  117.1 0.0 copy-done.2
  117.1 0.0 copy-start.3
  117.1 0.0 copy-start.4
  117.1 0.0 copy-start.5
  117.2 72.6 %join.2 = f32[32,64,384]{2,1,0:T(8,128)} custom-call(s32[128,128]{1,0:T(8,128)} %get-tuple-element.67.slot_ref, s32[128,128]{1,0:T(8,128)} %get-tuple-element.68.place_ref, s32[32,128]{1,0:T(8,128)} %get-tuple-element.69.count_ref, f32[128,128]{1,0:T(8,128)S(1)} %bitcast.24, f32[64,16384]{1,0:T(8,128)} %bitcast.18, f32[11264,128]{1,0:T(8,128)} %bitcast.22), custom_call_target="tpu_custom_call" | custom-call | tf_op jit(solution)/shard_map/join/pallas_call | solution.py:395
  189.7 0.0 copy-done.3
  189.7 0.0 copy-done.4
  189.7 0.0 copy-done.5
  189.7 0.7 while.12
  190.4 47.8 %reduce_factor.1 = f32[4,192,192]{2,1,0:T(8,128)} custom-call(f32[8,4,64,384]{3,2,1,0:T(8,128)} %bitcast.17), custom_call_target="tpu_custom_call" | custom-call | tf_op jit(solution)/shard_map/reduce_factor/pallas_call | solution.py:539
  238.3 2.1 copy.21
Async XLA Ops:
  0.0 117.1 %copy-start.2 = (f32[1,16384]{1,0:T(1,128)S(1)}, f32[1,16384]{1,0:T(1,128)}, u32[]{:S(2)}) copy-start(f32[1,16384]{1,0:T(1,128)} %param.10) | copy-start | bytes 196612
  33.2 1.4 copy-start
  117.1 72.6 %copy-start.3 = (s32[1,16384,1]{1,2,0:T(1,128)S(1)}, s32[1,16384,1]{1,2,0:T(1,128)}, u32[]{:S(2)}) copy-start(s32[1,16384,1]{1,2,0:T(1,128)} %param.11) | copy-start | bytes 196612
  117.1 72.6 %copy-start.4 = (s32[1,16384]{1,0:T(1,128)S(1)}, s32[1,16384]{1,0:T(1,128)}, u32[]{:S(2)}) copy-start(s32[1,16384]{1,0:T(1,128)} %param.12) | copy-start | bytes 196612
  117.1 72.6 %copy-start.5 = (s32[1,16384,1]{1,2,0:T(1,128)S(1)}, s32[1,16384,1]{1,2,0:T(1,128)}, u32[]{:S(2)}) copy-start(s32[1,16384,1]{1,2,0:T(1,128)} %param.13) | copy-start | bytes 196612

commit v6 on v5

--- a/solution.py
+++ b/solution.py
@@ -9,7 +9,6 @@
 
 UNITS = 32
 COEFFS = 64
-UCAP = 1024
 SKY = 16
 TM = 8
 DEVS = SKY * TM
@@ -20,7 +19,6 @@
 HALF = SLOTS // 2
 LINES = CLASSES * HALF
 BLOCK = 256
-DUMP = UNITS * UCAP
 F32 = jnp.float32
 BF16 = jnp.bfloat16
 I32 = jnp.int32
@@ -30,7 +28,8 @@
     return lax.dot_general(a, b, (dims, ((), ())), precision=precision, preferred_element_type=F32)
 
 
-def route_body(round_ref, owner_ref, row_ref, unit_ref, req_ref, slot_ref, place_ref, count_ref, acc_ref):
+def route_body(round_ref, owner_ref, row_ref, unit_ref, req_ref, epoch_ref, reply_ref, span_ref,
+               acc_ref, sort_ref, slot_ref, rank_ref):
     first = round_ref[0] * SLOTS
     tri_row = lax.broadcasted_iota(I32, (BLOCK, BLOCK + 128), 0)
     tri_col = lax.broadcasted_iota(I32, (BLOCK, BLOCK + 128), 1)
@@ -67,16 +66,41 @@
         mine = (units == unit) & active
         unit_ahead = dot(mine.astype(BF16), before, ((1,), (0,)))
         unit_rank = jnp.sum(jnp.where(mine, unit_ahead[:, :BLOCK] + wide(unit_base), 0.0), axis=0, keepdims=True)
-        place = jnp.where(active, unit * UCAP + unit_rank.astype(I32), DUMP) * 2
+        unit_rank = jnp.where(active, unit_rank.astype(I32), -2 * E_DEV)
         for half in range(2):
             lanes = slice(half * 128, half * 128 + 128)
             slot_ref[pl.ds(2 * b + half, 1), :] = slot[:, lanes]
-            place_ref[pl.ds(2 * b + half, 1), :] = place[:, lanes]
+            rank_ref[pl.ds(2 * b + half, 1), :] = unit_rank[:, lanes]
         return base + ahead[:, BLOCK:], unit_base + unit_ahead[:, BLOCK:]
 
     start = (jnp.zeros((CLASSES, 128), F32), jnp.zeros((UNITS, 128), F32))
     base, unit_base = lax.fori_loop(0, E_DEV // BLOCK, step, start, unroll=4)
-    count_ref[...] = unit_base.astype(I32)
+    ends = unit_base
+    unit_row = lax.broadcasted_iota(I32, (UNITS, 128), 0)
+    for shift in (1, 2, 4, 8, 16):
+        ends = ends + jnp.where(unit_row >= shift, pltpu.roll(ends, shift, 0), 0.0)
+    begins = ends - unit_base
+    span_ref[0:UNITS, :] = unit_base.astype(I32)
+    span_ref[UNITS:, :] = begins.astype(I32)
+    sort_ref[...] = jnp.zeros_like(sort_ref)
+    lines = lax.broadcasted_iota(I32, (128, BLOCK), 0)
+    lane = lax.broadcasted_iota(I32, (1, BLOCK), 1)
+
+    def sort(b, _):
+        slot, unit_rank, unit = pair(slot_ref, b), pair(rank_ref, b), pair(unit_ref, b)
+        begin = jnp.sum(jnp.where(units == unit, wide(begins), 0.0), axis=0, keepdims=True)
+        place = unit_rank + begin.astype(I32)
+        epoch = b * BLOCK + lane
+        hot = lines == (place >> 7)
+        pieces = (epoch >> 7, epoch & 127, slot >> 8, slot & 255)
+        values = jnp.concatenate([jnp.where(hot, v.astype(F32), 0.0) for v in pieces], axis=0).astype(BF16)
+        put = (lines == (place & 127)).astype(BF16)
+        sort_ref[...] += dot(values, put, ((1,), (1,)))
+        return _
+
+    lax.fori_loop(0, E_DEV // BLOCK, sort, 0, unroll=4)
+    epoch_ref[...] = (sort_ref[0:128, :] * 128.0 + sort_ref[128:256, :]).astype(I32)
+    reply_ref[...] = (sort_ref[256:384, :] * 256.0 + sort_ref[384:512, :]).astype(I32)
     more = (jnp.max(base).astype(I32) > first + SLOTS).astype(I32)
     wanted = (acc_ref[0:CLASSES, :] * 64.0 + acc_ref[CLASSES:, :]).astype(I32)
     req_ref[:, 0, :] = wanted[:, 0:128]
@@ -89,8 +113,14 @@
     jax.ShapeDtypeStruct((CLASSES, 4, 128), I32),
     jax.ShapeDtypeStruct((128, 128), I32),
     jax.ShapeDtypeStruct((128, 128), I32),
-    jax.ShapeDtypeStruct((UNITS, 128), I32),
+    jax.ShapeDtypeStruct((2 * UNITS, 128), I32),
 )
+ROUTE_SCRATCH = [
+    pltpu.VMEM((2 * CLASSES, SLOTS), F32),
+    pltpu.VMEM((512, 128), F32),
+    pltpu.VMEM((128, 128), I32),
+    pltpu.VMEM((128, 128), I32),
+]
 SMEM_SPEC = pl.BlockSpec(memory_space=pltpu.SMEM)
 VMEM_SPEC = pl.BlockSpec(memory_space=pltpu.VMEM)
 ANY_SPEC = pl.BlockSpec(memory_space=pl.ANY)
@@ -102,15 +132,12 @@
         out_shape=PLAN,
         in_specs=[SMEM_SPEC, VMEM_SPEC, VMEM_SPEC, VMEM_SPEC],
         out_specs=(VMEM_SPEC,) * 4,
-        scratch_shapes=[pltpu.VMEM((2 * CLASSES, SLOTS), F32)],
+        scratch_shapes=ROUTE_SCRATCH,
         name="route",
     )(number, owner, row, unit)
 
 
 MESH = pl.DeviceIdType.MESH
-TURN = 11
-
-
 def nearer(i):
     x, y, z = i % 4, i // 4 % 4, i // 16
     hops = min(x, 4 - x) + min(y, 4 - y) + z
@@ -145,10 +172,15 @@
     return ((z & 1) * 2 + core) * 16 + ((y + turned) & 3) * 4 + ((x + turned) & 3)
 
 
-def near_offset(k):
-    i = ((k >> 1) * TURN) & 31
+def turn_of(k):
+    step = 13 + 6 * (lax.axis_index("tm") & 1)
+    return ((k * step) & 31) + (k & 32)
+
+
+def near_offset(n):
+    i = n & 31
     flip = ((FLIPS >> i) & 1) * 2
-    return (i & 3) + flip, (i >> 2) + flip, (i >> 4) + flip, k & 1
+    return (i & 3) + flip, (i >> 2) + flip, (i >> 4) + flip, n >> 5
 
 
 def next_device(k):
@@ -157,7 +189,8 @@
 
 
 def prepare_kernel(round_ref, owner_ref, row_ref, unit_ref, tab_ref,
-                   table_ref, req_ref, slot_ref, place_ref, count_ref, acc_ref, send_sem, recv_sem):
+                   table_ref, req_ref, epoch_ref, reply_ref, span_ref, acc_ref, sort_ref, slot_ref, rank_ref,
+                   send_sem, recv_sem):
     here = position()
     x, y, z, core = here
     sky = y * 4 + x
@@ -187,7 +220,8 @@
 
     lax.fori_loop(1, SKY, give, 0)
     pltpu.make_async_copy(piece(here), table_ref.at[sky], recv_sem).start()
-    route_body(round_ref, owner_ref, row_ref, unit_ref, req_ref, slot_ref, place_ref, count_ref, acc_ref)
+    route_body(round_ref, owner_ref, row_ref, unit_ref, req_ref, epoch_ref, reply_ref, span_ref,
+               acc_ref, sort_ref, slot_ref, rank_ref)
     pltpu.make_async_copy(table_ref.at[pl.ds(0, SKY - 1)], table_ref.at[pl.ds(0, SKY - 1)], send_sem).wait()
     pltpu.make_async_copy(table_ref, table_ref, recv_sem).wait()
 
@@ -198,14 +232,15 @@
         out_shape=(jax.ShapeDtypeStruct((SKY, COEFFS, STRIPE), F32),) + PLAN,
         in_specs=[SMEM_SPEC, VMEM_SPEC, VMEM_SPEC, VMEM_SPEC, ANY_SPEC],
         out_specs=(VMEM_SPEC,) * 5,
-        scratch_shapes=[pltpu.VMEM((2 * CLASSES, SLOTS), F32)] + [pltpu.SemaphoreType.DMA] * 2,
+        scratch_shapes=ROUTE_SCRATCH + [pltpu.SemaphoreType.DMA] * 2,
         compiler_params=pltpu.CompilerParams(collective_id=2, has_side_effects=True),
         name="prepare",
     )(number, owner, row, unit, spectra)
 
 
-def exchange_kernel(req_ref, tab_ref, out_ref, more_ref, rows_ref, asked_ref, flag_ref, index_ref, send_ref,
-                    ask_send, ask_recv, flag_send, flag_recv, local, send_sem, recv_sem):
+def exchange_kernel(req_ref, tab_ref, epoch_ref, time_ref, obs_ref, out_ref, more_ref, sorted_ref,
+                    rows_ref, asked_ref, flag_ref, index_ref, send_ref, obs_here, local_ref, order_ref,
+                    obs_sem, sorted_sem, ask_send, ask_recv, flag_send, flag_recv, local, send_sem, recv_sem):
     here = position()
     mine = class_of(here)
     half_turn = (2, 2, 2, 0)
@@ -219,18 +254,22 @@
     lax.fori_loop(1, DEVS, greet, 0)
     pl.semaphore_wait(barrier, DEVS - 1)
 
+    obs_copy = pltpu.make_async_copy(obs_ref, obs_here, obs_sem)
+    obs_copy.start()
+
     def ask(k, _):
-        at = moved(here, near_offset(k))
+        n = turn_of(k)
+        at = moved(here, near_offset(n))
         pltpu.make_async_remote_copy(
-            src_ref=req_ref.at[class_of(at)], dst_ref=asked_ref.at[k], send_sem=ask_send, recv_sem=ask_recv,
+            src_ref=req_ref.at[class_of(at)], dst_ref=asked_ref.at[n], send_sem=ask_send, recv_sem=ask_recv,
             device_id=mesh_id(at), device_id_type=MESH,
         ).start()
         return _
 
-    def tell(k, _):
-        at = moved(moved(here, near_offset(k)), half_turn)
+    def tell(n, _):
+        at = moved(moved(here, near_offset(n)), half_turn)
         pltpu.make_async_remote_copy(
-            src_ref=req_ref.at[0], dst_ref=flag_ref.at[k], send_sem=flag_send, recv_sem=flag_recv,
+            src_ref=req_ref.at[0], dst_ref=flag_ref.at[n], send_sem=flag_send, recv_sem=flag_recv,
             device_id=mesh_id(at), device_id_type=MESH,
         ).start()
         return _
@@ -257,13 +296,14 @@
             send_ref[k, j : j + 1, :] = jnp.where(left, rows_ref[pl.ds(a, 1), :], rows_ref[pl.ds(b, 1), :])
 
     def send(k):
+        n = turn_of(k)
         pltpu.make_async_remote_copy(
-            src_ref=send_ref.at[k], dst_ref=out_ref.at[mine], send_sem=send_sem, recv_sem=recv_sem,
-            device_id=mesh_id(moved(here, [-o for o in near_offset(k)])), device_id_type=MESH,
+            src_ref=send_ref.at[n], dst_ref=out_ref.at[mine], send_sem=send_sem, recv_sem=recv_sem,
+            device_id=mesh_id(moved(here, [-o for o in near_offset(n)])), device_id_type=MESH,
         ).start()
 
     def serve(k, _):
-        gather(k)
+        gather(turn_of(k))
 
         @pl.when(k > 1)
         def _():
@@ -275,6 +315,39 @@
     gather(0)
     send(CLASSES - 1)
     pltpu.make_async_copy(send_ref.at[0], out_ref.at[mine], recv_sem).start()
+
+    obs_copy.wait()
+
+    def turn(b, _):
+        at = pl.multiple_of(b * 128, 128)
+        times = jnp.broadcast_to(time_ref[pl.ds(b, 1), :], (COEFFS, 128))
+        local_ref[pl.ds(at, 128), :] = jnp.concatenate([times, obs_here[:, pl.ds(at, 128)]], axis=0).T
+        return _
+
+    lax.fori_loop(0, 128, turn, 0)
+
+    def put_out(c):
+        part = pl.ds(pl.multiple_of(c * SORT_ROWS, SORT_ROWS), SORT_ROWS)
+        pltpu.make_async_copy(order_ref.at[part], sorted_ref.at[part], sorted_sem).start()
+
+    def pick(c, _):
+        def line(i, _):
+            at = pl.multiple_of(c * SORT_ROWS + i * 128, 128)
+            for j in range(128):
+                e = epoch_ref[c * (SORT_ROWS // 128) + i, j]
+                order_ref[pl.ds(at + j, 1), :] = local_ref[pl.ds(e, 1), :]
+            return _
+
+        lax.fori_loop(0, SORT_ROWS // 128, line, 0)
+
+        @pl.when(c > 0)
+        def _():
+            put_out(c - 1)
+
+        return 0
+
+    lax.fori_loop(0, E_DEV // SORT_ROWS, pick, 0)
+    put_out(E_DEV // SORT_ROWS - 1)
     most = slice(0, CLASSES - 1)
     pltpu.make_async_copy(asked_ref.at[most], asked_ref.at[most], ask_send).wait()
     pltpu.make_async_copy(flag_ref, flag_ref, flag_send).wait()
@@ -282,140 +355,116 @@
     more_ref[...] = jnp.maximum(jnp.max(asked_ref[:, 3, :], axis=0, keepdims=True),
                                 jnp.max(flag_ref[:, 3, :], axis=0, keepdims=True))
     pltpu.make_async_copy(send_ref.at[most], send_ref.at[most], send_sem).wait()
+    pltpu.make_async_copy(sorted_ref, sorted_ref, sorted_sem).wait()
     pltpu.make_async_copy(out_ref, out_ref, recv_sem).wait()
 
 
-def exchange(collective, requests, table):
+SORT_ROWS = 2048
+
+
+def exchange(collective, plan, table, times, obs):
     return pl.pallas_call(
         exchange_kernel,
         out_shape=(
             jax.ShapeDtypeStruct((CLASSES, HALF, 128), F32),
             jax.ShapeDtypeStruct((1, 128), I32),
+            jax.ShapeDtypeStruct((E_DEV, 128), F32),
         ),
-        in_specs=[VMEM_SPEC, VMEM_SPEC],
-        out_specs=(ANY_SPEC, VMEM_SPEC),
+        in_specs=[VMEM_SPEC, VMEM_SPEC, SMEM_SPEC, VMEM_SPEC, ANY_SPEC],
+        out_specs=(ANY_SPEC, VMEM_SPEC, ANY_SPEC),
         scratch_shapes=[
             pltpu.VMEM((SKY * STRIPE, 128), F32),
             pltpu.VMEM((CLASSES, 4, 128), I32),
             pltpu.VMEM((CLASSES, 4, 128), I32),
             pltpu.SMEM((CLASSES, 4, 128), I32),
             pltpu.VMEM((CLASSES, HALF, 128), F32),
-        ] + [pltpu.SemaphoreType.DMA] * 7,
+            pltpu.VMEM((COEFFS, E_DEV), F32),
+            pltpu.VMEM((E_DEV, 128), F32),
+            pltpu.VMEM((E_DEV, 128), F32),
+        ] + [pltpu.SemaphoreType.DMA] * 9,
         compiler_params=pltpu.CompilerParams(collective_id=collective, has_side_effects=True),
         name="exchange",
-    )(requests, table)
-
-
-JOIN_STEPS = 8
-JOIN_BLOCKS = 128 // JOIN_STEPS
-
-
-def join_kernel(scale, slot_ref, place_ref, count_ref, time_ref, obs_ref, reply_ref, *refs):
-    *old_ref, out_ref, rows_ref, x_ref, block_ref, sums_ref, sem, old_sem = refs
-    step = pl.program_id(0)
-
-    @pl.when(step == 0)
-    def _():
-        copy = pltpu.make_async_copy(reply_ref, rows_ref.at[pl.ds(0, LINES), :], sem)
-        copy.start()
-
-        for old in old_ref:
-            before = pltpu.make_async_copy(old, out_ref, old_sem)
-            before.start()
-            before.wait()
-        copy.wait()
-
-        def turn(i, _):
-            at = pl.multiple_of(i * 256, 256)
-            rows_ref[pl.ds(LINES + at, 256), :] = pltpu.roll(rows_ref[pl.ds(at, 256), :], COEFFS, 1)
+    )(plan[0], table, plan[1], times, obs)
+
+
+def join_kernel(scale, line_ref, span_ref, reply_ref, sorted_ref, *refs):
+    *old_ref, out_ref, rows_ref, picked_ref, local_ref, sums_ref, sem, local_sem, old_sem = refs
+    copy = pltpu.make_async_copy(reply_ref, rows_ref.at[pl.ds(0, LINES), :], sem)
+    copy.start()
+    local_copy = pltpu.make_async_copy(sorted_ref, local_ref.at[pl.ds(0, E_DEV), :], local_sem)
+    local_copy.start()
+    for old in old_ref:
+        before = pltpu.make_async_copy(old, out_ref, old_sem)
+        before.start()
+        before.wait()
+    copy.wait()
+
+    def turn(i, _):
+        at = pl.multiple_of(i * 256, 256)
+        rows_ref[pl.ds(LINES + at, 256), :] = pltpu.roll(rows_ref[pl.ds(at, 256), :], COEFFS, 1)
+        return _
+
+    lax.fori_loop(0, LINES // 256, turn, 0)
+
+    def pick(c, _):
+        at = pl.multiple_of(c * 128, 128)
+        for j in range(128):
+            picked_ref[pl.ds(at + j, 1), :] = rows_ref[pl.ds(line_ref[c, j], 1), :]
+        return _
+
+    lax.fori_loop(0, E_DEV // 128, pick, 0)
+    local_copy.wait()
+    left = lax.broadcasted_iota(I32, (1, 128), 1) < COEFFS
+
+    def put(u, at, value):
+        lanes = slice(at, at + 128)
+        out_ref[u, :, lanes] = out_ref[u, :, lanes] + value if old_ref else value
+
+    def unit_gram(u, _):
+        count = span_ref[u, 0]
+        begin = span_ref[UNITS + u, 0]
+        sums_ref[...] = jnp.zeros_like(sums_ref)
+
+        def add(i, _):
+            part = pl.ds(begin + i * 256, 256)
+            ref, own = picked_ref[part, :], local_ref[part, :]
+            x = jnp.concatenate([jnp.where(left, ref, own), ref * own], axis=1)
+            rows = lax.broadcasted_iota(I32, (256, 256), 0) + i * 256
+            x = jnp.where(rows < count, x, 0.0)
+            high = x.astype(BF16)
+            low = (x - high.astype(F32)).astype(BF16)
+            sums_ref[...] += dot(high, jnp.concatenate([high, low], axis=1), ((0,), (0,)))
             return _
 
-        lax.fori_loop(0, LINES // 256, turn, 0)
-
-    left = lax.broadcasted_iota(I32, (1, 128), 1) < COEFFS
-
-    def place_block(k, _):
-        b = step * JOIN_BLOCKS + k
-        at = pl.multiple_of(k * 128, 128)
-        times = jnp.broadcast_to(time_ref[pl.ds(b, 1), :], (COEFFS, 128))
-        plain = jnp.concatenate([jnp.ones((COEFFS, 128), F32), obs_ref[:, pl.ds(at, 128)]], axis=0)
-        timed = jnp.concatenate([times, jnp.zeros((COEFFS, 128), F32)], axis=0)
-        block_ref[pl.ds(0, 128, stride=2), :] = plain.T
-        block_ref[pl.ds(1, 128, stride=2), :] = timed.T
-        for j in range(128):
-            s = slot_ref[b, j]
-            p = place_ref[b, j]
-            r = rows_ref[pl.ds(s, 2, stride=0), :]
-            o = block_ref[2 * j : 2 * j + 2, :]
-            x_ref[pl.ds(p, 2), :] = jnp.where(left, r * o, o)
-        return _
-
-    lax.fori_loop(0, JOIN_BLOCKS, place_block, 0)
-
-    @pl.when(step == JOIN_STEPS - 1)
-    def _():
-        def put(u, at, value):
-            lanes = slice(at, at + 128)
-            out_ref[u, :, lanes] = out_ref[u, :, lanes] + value if old_ref else value
-
-        def unit_gram(u, _):
-            count = count_ref[u, 0]
-            sums_ref[...] = jnp.zeros_like(sums_ref)
-
-            def add(i, _):
-                at = pl.multiple_of(u * UCAP + i * 256, 256)
-                x = jnp.concatenate(
-                    [x_ref[pl.ds(2 * at, 256, stride=2), :], x_ref[pl.ds(2 * at + 1, 256, stride=2), :]], axis=1
-                )
-                rows = lax.broadcasted_iota(I32, (256, 256), 0) + i * 256
-                x = jnp.where(rows < count, x, 0.0)
-                high = x.astype(BF16)
-                low = (x - high.astype(F32)).astype(BF16)
-                sums_ref[...] += dot(high, jnp.concatenate([high, low], axis=1), ((0,), (0,)))
-                return _
-
-            lax.fori_loop(0, (count + 255) // 256, add, 0)
-            cross = sums_ref[:, 256:]
-            gram = (sums_ref[:, :256] + cross + cross.T) * scale
-            turned = pltpu.roll(gram, COEFFS, 1)
-            ref = slice(0, 64)
-            obs = slice(64, 128)
-            tim = slice(128, 192)
-            put(u, 0, jnp.where(left, gram[ref, 0:128], turned[ref, 128:256]))
-            put(u, 128, jnp.where(left, turned[ref, 128:256], turned[tim, 128:256]))
-            put(u, 256, jnp.where(left, turned[tim, 128:256], gram[obs, 0:128]))
-            return _
-
-        lax.fori_loop(0, UNITS, unit_gram, 0)
-
-
-def join(plan, times, obs, reply, scale, *old):
-    smem = pl.BlockSpec(memory_space=pltpu.SMEM)
-    once = functools.partial(pl.BlockSpec, pipeline_mode=pl.Buffered(1))
+        lax.fori_loop(0, (count + 255) // 256, add, 0)
+        cross = sums_ref[:, 256:]
+        gram = (sums_ref[:, :256] + cross + cross.T) * scale
+        turned = pltpu.roll(gram, COEFFS, 1)
+        ref = slice(0, 64)
+        obs = slice(64, 128)
+        tim = slice(128, 192)
+        put(u, 0, jnp.where(left, gram[ref, 0:128], turned[ref, 128:256]))
+        put(u, 128, jnp.where(left, turned[ref, 128:256], turned[tim, 128:256]))
+        put(u, 256, jnp.where(left, turned[tim, 128:256], gram[obs, 0:128]))
+        return _
+
+    lax.fori_loop(0, UNITS, unit_gram, 0)
+
+
+def join(plan, replies, local, scale, *old):
     return pl.pallas_call(
         functools.partial(join_kernel, scale),
-        grid=(JOIN_STEPS,),
         out_shape=jax.ShapeDtypeStruct((UNITS, COEFFS, 384), F32),
-        in_specs=[
-            smem,
-            smem,
-            smem,
-            once((128, 128), lambda i: (0, 0)),
-            pl.BlockSpec((COEFFS, JOIN_BLOCKS * 128), lambda i: (0, i)),
-            ANY_SPEC,
-        ] + [ANY_SPEC] * len(old),
-        out_specs=once((UNITS, COEFFS, 384), lambda i: (0, 0, 0)),
+        in_specs=[SMEM_SPEC, SMEM_SPEC, ANY_SPEC, ANY_SPEC] + [ANY_SPEC] * len(old),
+        out_specs=VMEM_SPEC,
         scratch_shapes=[
-            pltpu.VMEM((2 * LINES + 8, 128), F32),
-            pltpu.VMEM((2 * DUMP + 8, 128), F32),
-            pltpu.VMEM((256, 128), F32),
+            pltpu.VMEM((2 * LINES, 128), F32),
+            pltpu.VMEM((E_DEV + 256, 128), F32),
+            pltpu.VMEM((E_DEV + 256, 128), F32),
             pltpu.VMEM((256, 512), F32),
-            pltpu.SemaphoreType.DMA,
-            pltpu.SemaphoreType.DMA,
-        ],
-        compiler_params=pltpu.CompilerParams(vmem_limit_bytes=62 << 20),
+        ] + [pltpu.SemaphoreType.DMA] * 3,
         name="join",
-    )(*plan[1:], times, obs, reply.reshape(LINES, 128), *old)
+    )(plan[2], plan[3], replies.reshape(LINES, 128), local, *old)
 
 
 PANEL = 32
@@ -444,24 +493,14 @@
     def step(i, _):
         at = pl.multiple_of(i * PANEL, PANEL)
         panels = [pltpu.roll(work_ref[m, pl.ds(at, PANEL), :], 256 - at, 1) for m in range(QUAD)]
-        for k in range(0, PANEL - 2, 2):
+        for k in range(PANEL - 1):
             for m in range(QUAD):
                 panel = panels[m]
-                p, q = panel[k : k + 1, :], panel[k + 1 : k + 2, :]
-                a, b, c = p[:, k : k + 1], p[:, k + 1 : k + 2], q[:, k + 1 : k + 2]
-                inverse = 1.0 / (a * c - b * b)
-                u = (c * inverse) * p - (b * inverse) * q
-                v = (a * inverse) * q - (b * inverse) * p
-                left = jnp.where(thin > k + 1, panel[:, k : k + 1], 0.0)
-                right = jnp.where(thin > k + 1, panel[:, k + 1 : k + 2], 0.0)
-                panels[m] = panel - left * u - right * v
+                pivot = 1.0 / panel[k : k + 1, k : k + 1]
+                below = jnp.where(thin > k, panel[:, k : k + 1] * pivot, 0.0)
+                panels[m] = panel - below * panel[k : k + 1, :]
         for m in range(QUAD):
             panel = panels[m]
-            above = pltpu.roll(panel, 1, 0)
-            b = jnp.sum(jnp.where(col == row, above, 0.0), axis=1, keepdims=True)
-            a = jnp.sum(jnp.where(col == row - 1, above, 0.0), axis=1, keepdims=True)
-            second = (thin & 1) == 1
-            panel = panel - jnp.where(second, b / jnp.where(second, a, 1.0), 0.0) * above
             diag = jnp.sum(jnp.where(col == row, panel, 0.0), axis=1, keepdims=True)
             panel = jnp.where((col >= row) & (col < 192 - at), panel * (1.0 / jnp.sqrt(diag)), 0.0)
             panel = pltpu.roll(panel, at, 1)
@@ -567,15 +606,15 @@
     number = jnp.zeros((1,), I32)
     table, *plan = prepare(number, owners, rows, units, reference_spectra.T)
 
-    replies, more = exchange(0, plan[0], table)
-    gram = join(plan, times, obs, replies, scale)
+    replies, more, local = exchange(0, plan, table, times, obs)
+    gram = join(plan, replies, local, scale)
 
     def next_round(state):
         number, _, gram = state
         number = number + 1
         plan = route(number, owners, rows, units)
-        replies, more = exchange(3, plan[0], table)
-        return number, more, join(plan, times, obs, replies, scale, gram)
+        replies, more, local = exchange(3, plan, table, times, obs)
+        return number, more, join(plan, replies, local, scale, gram)
 
     gram = lax.while_loop(lambda state: state[1][0, 0] > 0, next_round, (number, more, gram))[2]
     return reduce_factor(gram)[None]

time: 243 us -> 195 us (0.80); the launches traced: 240 us -> 196 us
  Pallas kernels: 236 us -> 193 us
    pallas_call x1, Pallas kernels: 72.6 us -> 50.6 us  [join(): pl.pallas_call(functools.partial(join_kernel, scale), out_shape=jax.Shape...]
    pallas_call x1, Pallas kernels: 82.5 us -> 68.6 us  [exchange(): pl.pallas_call(exchange_kernel, out_shape=(jax.ShapeDtypeStruct((CLASSES,...]
    pallas_call x1, Pallas kernels: 47.8 us -> 40 us  [reduce_factor(): pl.pallas_call(reduce_kernel, out_shape=jax.ShapeDtypeStruct((QUAD, 192,...]
where the time goes in v6:
time: 195 us; the launch traced here: 196 us
  Pallas kernels  193 us (99%)
  local copies, waits for them, and re-layouts  2.09 us (1%)
    pallas_call x1, Pallas kernels, exchange(): pl.pallas_call(exchange_kernel, out_shape=(jax.ShapeDtypeStruct((CLASSES,...  68.6 us
    pallas_call x1, Pallas kernels, join(): pl.pallas_call(functools.partial(join_kernel, scale), out_shape=jax.Shape...  50.6 us
    pallas_call x1, Pallas kernels, reduce_factor(): pl.pallas_call(reduce_kernel, out_shape=jax.ShapeDtypeStruct((QUAD, 192,...  40 us
    pallas_call x1, Pallas kernels, prepare(): pl.pallas_call(prepare_kernel, out_shape=(jax.ShapeDtypeStruct((SKY, COEF...  33.5 us

profile of v6, /device:TPU:1, one launch (start us, length us, event | category | flops | bytes accessed | tf_op | source)
XLA Modules:
  0.0 195.6 jit_solution(4919138640251359536)
XLA Ops:
  0.0 0.0 copy-start.1
  0.0 33.5 %prepare.1 = (f32[16,64,512]{2,1,0:T(8,128)S(1)}, s32[64,4,128]{2,1,0:T(4,128)}, s32[128,128]{1,0:T(8,128)}, s32[128,128]{1,0:T(8,128)}, s32[64,128]{1,0:T(8,128)}) custom-call(s32[1]{0:T(128)} %copy.19.round_ref, s32[128,128]{1,0:T(8,128)} %bitcast.26, s32[128,128]{1,0:T(8,128)} %bitcast.28, s32[128,128]{1,0:T(8,128)} %bitcast.30, f32[64,32768]{1,0:T(8,128)} %bitcast.21), custom_call_target="tpu_custom_call" | custom-call | tf_op jit(solution)/shard_map/prepare/pallas_call | solution.py:230
  33.5 0.0 copy-start
  33.5 0.0 copy-done.1
  33.5 68.6 %exchange.2 = (f32[64,176,128]{2,1,0:T(8,128)}, s32[1,128]{1,0:T(1,128)}, f32[16384,128]{1,0:T(8,128)}) custom-call(s32[64,4,128]{2,1,0:T(4,128)} %get-tuple-element.66.req_ref, f32[16,64,512]{2,1,0:T(8,128)S(1)} %get-tuple-element.151.tab_ref, s32[128,128]{1,0:T(8,128)} %get-tuple-element.68.epoch_ref, f32[128,128]{1,0:T(8,128)S(1)} %bitcast.24, ...), custom_call_target="tpu_custom_call" | custom-call | tf_op jit(solution)/shard_map/exchange/pallas_call | solution.py:366
  102.2 0.0 copy-done
  102.2 0.0 copy-start.2
  102.2 0.0 copy-start.3
  102.2 0.0 copy-start.4
  102.2 50.6 %join.2 = f32[32,64,384]{2,1,0:T(8,128)S(1)} custom-call(s32[128,128]{1,0:T(8,128)} %get-tuple-element.70.line_ref, s32[64,128]{1,0:T(8,128)} %get-tuple-element.71.span_ref, f32[11264,128]{1,0:T(8,128)} %bitcast.22, f32[16384,128]{1,0:T(8,128)} %get-tuple-element.73.sorted_ref), custom_call_target="tpu_custom_call" | custom-call | tf_op jit(solution)/shard_map/join/pallas_call | solution.py:455
  152.9 0.0 copy-done.2
  152.9 0.0 copy-done.3
  152.9 0.0 copy-done.4
  152.9 0.6 while.12
  153.5 40.0 %reduce_factor.1 = f32[4,192,192]{2,1,0:T(8,128)} custom-call(f32[8,4,64,384]{3,2,1,0:T(8,128)S(1)} %bitcast.17), custom_call_target="tpu_custom_call" | custom-call | tf_op jit(solution)/shard_map/reduce_factor/pallas_call | solution.py:578
  193.5 2.1 %copy.21 = f32[1,4,192,192]{3,2,1,0:T(8,128)} copy(f32[1,4,192,192]{3,2,1,0:T(8,128)} %bitcast.23) | data formatting | bytes 1179648
Async XLA Ops:
  0.0 33.5 %copy-start.1 = (f32[1,16384]{1,0:T(1,128)S(1)}, f32[1,16384]{1,0:T(1,128)}, u32[]{:S(2)}) copy-start(f32[1,16384]{1,0:T(1,128)} %param.10) | copy-start | bytes 196612
  33.5 68.7 %copy-start = (f32[16,64,512]{2,1,0:T(8,128)}, f32[16,64,512]{2,1,0:T(8,128)S(1)}, u32[]{:S(2)}) copy-start(f32[16,64,512]{2,1,0:T(8,128)S(1)} %get-tuple-element.151.tab_ref) | copy-start | bytes 6291460
  102.2 50.7 %copy-start.2 = (s32[1,16384,1]{1,2,0:T(1,128)S(1)}, s32[1,16384,1]{1,2,0:T(1,128)}, u32[]{:S(2)}) copy-start(s32[1,16384,1]{1,2,0:T(1,128)} %param.11) | copy-start | bytes 196612
  102.2 50.7 %copy-start.3 = (s32[1,16384]{1,0:T(1,128)S(1)}, s32[1,16384]{1,0:T(1,128)}, u32[]{:S(2)}) copy-start(s32[1,16384]{1,0:T(1,128)} %param.12) | copy-start | bytes 196612
  102.2 50.7 %copy-start.4 = (s32[1,16384,1]{1,2,0:T(1,128)S(1)}, s32[1,16384,1]{1,2,0:T(1,128)}, u32[]{:S(2)}) copy-start(s32[1,16384,1]{1,2,0:T(1,128)} %param.13) | copy-start | bytes 196612

commit v7 on v6

--- a/solution.py
+++ b/solution.py
@@ -28,6 +28,10 @@
     return lax.dot_general(a, b, (dims, ((), ())), precision=precision, preferred_element_type=F32)
 
 
+def exact(small):
+    return small.astype(F32).astype(BF16)
+
+
 def route_body(round_ref, owner_ref, row_ref, unit_ref, req_ref, epoch_ref, reply_ref, span_ref,
                acc_ref, sort_ref, slot_ref, rank_ref):
     first = round_ref[0] * SLOTS
@@ -51,16 +55,15 @@
         group = row >> 9
         local = (owner << 9) + (row & (STRIPE - 1))
         hot = classes == group
-        ahead = dot(hot.astype(BF16), before, ((1,), (0,)))
+        hot_one = hot.astype(BF16)
+        ahead = dot(hot_one, before, ((1,), (0,)))
         rank = jnp.sum(jnp.where(hot, ahead[:, :BLOCK] + wide(base), 0.0), axis=0, keepdims=True)
         rank = rank.astype(I32) - first
         active = (rank >= 0) & (rank < SLOTS)
         upper = jnp.where(rank >= HALF, 1, 0)
         slot = upper * LINES + group * HALF + rank - upper * HALF
         slot = jnp.where(active, slot, 0)
-        high = (local >> 6).astype(F32)
-        low = (local & 63).astype(F32)
-        values = jnp.concatenate([jnp.where(hot, high, 0.0), jnp.where(hot, low, 0.0)], axis=0).astype(BF16)
+        values = jnp.concatenate([hot_one * exact(local >> 6), hot_one * exact(local & 63)], axis=0)
         put = (ranks == rank).astype(BF16)
         acc_ref[...] += dot(values, put, ((1,), (1,)))
         mine = (units == unit) & active
@@ -91,9 +94,9 @@
         begin = jnp.sum(jnp.where(units == unit, wide(begins), 0.0), axis=0, keepdims=True)
         place = unit_rank + begin.astype(I32)
         epoch = b * BLOCK + lane
-        hot = lines == (place >> 7)
+        hot_one = (lines == (place >> 7)).astype(BF16)
         pieces = (epoch >> 7, epoch & 127, slot >> 8, slot & 255)
-        values = jnp.concatenate([jnp.where(hot, v.astype(F32), 0.0) for v in pieces], axis=0).astype(BF16)
+        values = jnp.concatenate([hot_one * exact(v) for v in pieces], axis=0)
         put = (lines == (place & 127)).astype(BF16)
         sort_ref[...] += dot(values, put, ((1,), (1,)))
         return _
@@ -406,13 +409,13 @@
 
     lax.fori_loop(0, LINES // 256, turn, 0)
 
-    def pick(c, _):
-        at = pl.multiple_of(c * 128, 128)
-        for j in range(128):
-            picked_ref[pl.ds(at + j, 1), :] = rows_ref[pl.ds(line_ref[c, j], 1), :]
-        return _
-
-    lax.fori_loop(0, E_DEV // 128, pick, 0)
+    def pick(c):
+        at = pl.multiple_of(c * 256, 256)
+        for j in range(256):
+            picked_ref[pl.ds(at + j, 1), :] = rows_ref[pl.ds(line_ref[c * 2 + j // 128, j % 128], 1), :]
+
+    pick(0)
+    pick(1)
     local_copy.wait()
     left = lax.broadcasted_iota(I32, (1, 128), 1) < COEFFS
 
@@ -420,33 +423,44 @@
         lanes = slice(at, at + 128)
         out_ref[u, :, lanes] = out_ref[u, :, lanes] + value if old_ref else value
 
-    def unit_gram(u, _):
+    def unit_gram(u, done):
         count = span_ref[u, 0]
         begin = span_ref[UNITS + u, 0]
         sums_ref[...] = jnp.zeros_like(sums_ref)
 
-        def add(i, _):
+        def add(i, to_pick):
             part = pl.ds(begin + i * 256, 256)
             ref, own = picked_ref[part, :], local_ref[part, :]
-            x = jnp.concatenate([jnp.where(left, ref, own), ref * own], axis=1)
-            rows = lax.broadcasted_iota(I32, (256, 256), 0) + i * 256
-            x = jnp.where(rows < count, x, 0.0)
-            high = x.astype(BF16)
-            low = (x - high.astype(F32)).astype(BF16)
-            sums_ref[...] += dot(high, jnp.concatenate([high, low], axis=1), ((0,), (0,)))
-            return _
-
-        lax.fori_loop(0, (count + 255) // 256, add, 0)
-        cross = sums_ref[:, 256:]
-        gram = (sums_ref[:, :256] + cross + cross.T) * scale
-        turned = pltpu.roll(gram, COEFFS, 1)
-        ref = slice(0, 64)
-        obs = slice(64, 128)
-        tim = slice(128, 192)
-        put(u, 0, jnp.where(left, gram[ref, 0:128], turned[ref, 128:256]))
-        put(u, 128, jnp.where(left, turned[ref, 128:256], turned[tim, 128:256]))
-        put(u, 256, jnp.where(left, turned[tim, 128:256], gram[obs, 0:128]))
-        return _
+            alive = lax.broadcasted_iota(I32, (256, 128), 0) + i * 256 < count
+            plain = jnp.where(alive, jnp.where(left, ref, own), 0.0)
+            timed = jnp.where(alive & left, ref * own, 0.0)
+            plain_high, timed_high = plain.astype(BF16), timed.astype(BF16)
+            plain_low = (plain - plain_high.astype(F32)).astype(BF16)
+            timed_both = timed_high.astype(F32) + pltpu.roll(timed - timed_high.astype(F32), COEFFS, 1)
+            high = jnp.concatenate([plain_high, timed_high], axis=1)[:, :192]
+            both = jnp.concatenate([plain_high, plain_low, timed_both.astype(BF16)], axis=1)
+            if to_pick is not None:
+                pick(to_pick)
+            sums_ref[...] += dot(high, both, ((0,), (0,)))
+
+        def add_block(i, done):
+            pl.when(done + 2 < E_DEV // 256)(lambda: add(i, done + 2))
+            pl.when(done + 2 >= E_DEV // 256)(lambda: add(i, None))
+            return done + 1
+
+        done = lax.fori_loop(0, (count + 255) >> 8, add_block, done)
+        sums = sums_ref[...] * scale
+        near, cross, late = sums[:, 0:128], sums[:, 128:256], sums[:, 256:384]
+        cross_t, late_t = cross.T, late.T
+        corner = near[0:128] + cross[0:128] + cross_t[:, 0:128]
+        late_sum = late[:, 0:64] + late[:, 64:128]
+        ref_tim = late_sum[0:64] + cross_t[0:64, 128:192]
+        tim_tim = late_sum[128:192] + late_t[64:128, 128:192]
+        tim_obs = near[128:192, 64:128] + cross[128:192, 64:128] + late_t[64:128, 64:128]
+        put(u, 0, jnp.concatenate([corner[0:64, 0:64], ref_tim], axis=1))
+        put(u, 128, jnp.concatenate([corner[0:64, 64:128], tim_tim], axis=1))
+        put(u, 256, jnp.concatenate([tim_obs, corner[64:128, 64:128]], axis=1))
+        return done
 
     lax.fori_loop(0, UNITS, unit_gram, 0)
 
@@ -461,13 +475,13 @@
             pltpu.VMEM((2 * LINES, 128), F32),
             pltpu.VMEM((E_DEV + 256, 128), F32),
             pltpu.VMEM((E_DEV + 256, 128), F32),
-            pltpu.VMEM((256, 512), F32),
+            pltpu.VMEM((192, 384), F32),
         ] + [pltpu.SemaphoreType.DMA] * 3,
         name="join",
     )(plan[2], plan[3], replies.reshape(LINES, 128), local, *old)
 
 
-PANEL = 32
+PANEL = 16
 QUAD = UNITS // TM
 
 
@@ -481,38 +495,49 @@
     return dot(one, two, ((0,), (0,)))
 
 
-def factor(gram, out_ref, work_ref):
-    work_ref[...] = jnp.zeros_like(work_ref)
-    work_ref[:, 0:64, 0:192] = gram[:, :, 0:192]
-    work_ref[:, 64:128, 64:192] = gram[:, :, 192:320]
-    work_ref[:, 128:192, 128:192] = gram[:, :, 320:384]
-    row = lax.broadcasted_iota(I32, (PANEL, 256), 0)
-    col = lax.broadcasted_iota(I32, (PANEL, 256), 1)
-    thin = lax.broadcasted_iota(I32, (PANEL, 1), 0)
-
-    def step(i, _):
-        at = pl.multiple_of(i * PANEL, PANEL)
-        panels = [pltpu.roll(work_ref[m, pl.ds(at, PANEL), :], 256 - at, 1) for m in range(QUAD)]
-        for k in range(PANEL - 1):
-            for m in range(QUAD):
-                panel = panels[m]
-                pivot = 1.0 / panel[k : k + 1, k : k + 1]
-                below = jnp.where(thin > k, panel[:, k : k + 1] * pivot, 0.0)
-                panels[m] = panel - below * panel[k : k + 1, :]
+def factor(gram, out_ref, work_ref, panel_ref):
+    def rows_of(m, first, many):
+        return pl.ds(first * QUAD + m, many, stride=QUAD)
+
+    def zeros(rows, lanes):
+        return jnp.zeros((rows, lanes), F32)
+
+    for m in range(QUAD):
+        for n, (lo, hi) in enumerate(((0, 192), (192, 320), (320, 384))):
+            parts = [gram[m, :, lo:hi], zeros(64, 64)]
+            block = jnp.concatenate([zeros(64, 64 * n)] * (n > 0) + parts, axis=1)
+            for tile in range(2):
+                work_ref[tile, rows_of(m, 64 * n, 64), :] = block[:, tile * 128 : tile * 128 + 128]
+
+    for start in range(0, 192, PANEL):
+        tiles = range(start // 128, 2)
+        lane0 = tiles[0] * 128
+        lane = lax.broadcasted_iota(I32, (QUAD, 256 - lane0), 1)
+        here = [slice((start + i) * QUAD, (start + i + 1) * QUAD) for i in range(PANEL)]
+        rows = [jnp.concatenate([work_ref[t, at, :] for t in tiles], axis=1) for at in here]
+        for k in range(PANEL):
+            at = start + k - lane0
+            head = rows[k]
+            pivot = head[:, at : at + 1]
+            scaled = head * (1.0 / pivot)
+            for i in range(k + 1, PANEL):
+                rows[i] = rows[i] - head[:, at + i - k : at + i - k + 1] * scaled
+            done = jnp.where(lane >= at, head * (1.0 / jnp.sqrt(pivot)), 0.0)
+            for t in tiles:
+                panel_ref[t, k * QUAD : (k + 1) * QUAD, :] = done[:, t * 128 - lane0 : t * 128 - lane0 + 128]
+        after = start + PANEL
         for m in range(QUAD):
-            panel = panels[m]
-            diag = jnp.sum(jnp.where(col == row, panel, 0.0), axis=1, keepdims=True)
-            panel = jnp.where((col >= row) & (col < 192 - at), panel * (1.0 / jnp.sqrt(diag)), 0.0)
-            panel = pltpu.roll(panel, at, 1)
-            out_ref[m, pl.ds(at, PANEL), :] = panel[:, :192]
-            update = square(panel)
-            work_ref[m] = work_ref[m] - update[:192, :]
-        return _
-
-    lax.fori_loop(0, 192 // PANEL, step, 0)
-
-
-def reduce_kernel(gram_ref, out_ref, pair_ref, sum_ref, part_ref, relay_ref, work_ref,
+            panel = jnp.concatenate([panel_ref[t, rows_of(m, 0, PANEL), :] for t in tiles], axis=1)
+            done = panel[:, : 192 - lane0]
+            out_ref[m, start:after, :] = done if lane0 == 0 else jnp.concatenate([zeros(PANEL, lane0), done], axis=1)
+            if after < 192:
+                update = square(panel)[after - lane0 : 192 - lane0, :]
+                rest = rows_of(m, after, 192 - after)
+                for t in tiles:
+                    work_ref[t, rest, :] = work_ref[t, rest, :] - update[:, t * 128 - lane0 : t * 128 - lane0 + 128]
+
+
+def reduce_kernel(gram_ref, out_ref, pair_ref, sum_ref, part_ref, relay_ref, work_ref, panel_ref,
                   pair_send, pair_recv, ring_send, ring_recv):
     sky, tm = lax.axis_index("sky"), lax.axis_index("tm")
     z, core = tm // 2, lax.rem(tm, 2)
@@ -570,7 +595,7 @@
     total = jnp.concatenate([sum_ref[z, 0:2] + part_ref[4], sum_ref[z, 2:4] + part_ref[5]], axis=0)
     for copy in (*pairs, far_up, far_down, near_up, near_down, last_up, last_down):
         copy.wait_send()
-    factor(total, out_ref, work_ref)
+    factor(total, out_ref, work_ref, panel_ref)
 
 
 def reduce_factor(gram):
@@ -585,7 +610,8 @@
             pltpu.VMEM((4, QUAD, COEFFS, 384), F32),
             pltpu.VMEM((6, 2, COEFFS, 384), F32),
             pltpu.VMEM((2, 2, COEFFS, 384), F32),
-            pltpu.VMEM((QUAD, 192, 256), F32),
+            pltpu.VMEM((2, 192 * QUAD, 128), F32),
+            pltpu.VMEM((2, PANEL * QUAD, 128), F32),
             pltpu.SemaphoreType.DMA((4,)),
             pltpu.SemaphoreType.DMA((4,)),
             pltpu.SemaphoreType.DMA((6,)),

time: 195 us -> 185 us (0.949)
  Pallas kernels: 193 us -> 182 us
    pallas_call x1, Pallas kernels: 50.6 us -> 41 us  [join(): pl.pallas_call(functools.partial(join_kernel, scale), out_shape=jax.Shape...]
where the time goes in v7:
time: 185 us
  Pallas kernels  182 us (98%)
  local copies, waits for them, and re-layouts  2.09 us (1%)
    pallas_call x1, Pallas kernels, exchange(): pl.pallas_call(exchange_kernel, out_shape=(jax.ShapeDtypeStruct((CLASSES,...  68.6 us
    pallas_call x1, Pallas kernels, join(): pl.pallas_call(functools.partial(join_kernel, scale), out_shape=jax.Shape...  41 us
    pallas_call x1, Pallas kernels, reduce_factor(): pl.pallas_call(reduce_kernel, out_shape=jax.ShapeDtypeStruct((QUAD, 192,...  38.6 us
    pallas_call x1, Pallas kernels, prepare(): pl.pallas_call(prepare_kernel, out_shape=(jax.ShapeDtypeStruct((SKY, COEF...  33.5 us

profile of v7, /device:TPU:1, one launch (start us, length us, event | category | flops | bytes accessed | tf_op | source)
XLA Modules:
  0.0 184.8 jit_solution(15115275948662452657)
XLA Ops:
  0.0 0.0 copy-start.1
  0.0 33.5 %prepare.1 = (f32[16,64,512]{2,1,0:T(8,128)S(1)}, s32[64,4,128]{2,1,0:T(4,128)}, s32[128,128]{1,0:T(8,128)}, s32[128,128]{1,0:T(8,128)}, s32[64,128]{1,0:T(8,128)}) custom-call(s32[1]{0:T(128)} %copy.19.round_ref, s32[128,128]{1,0:T(8,128)} %bitcast.26, s32[128,128]{1,0:T(8,128)} %bitcast.28, s32[128,128]{1,0:T(8,128)} %bitcast.30, f32[64,32768]{1,0:T(8,128)} %bitcast.21), custom_call_target="tpu_custom_call" | custom-call | tf_op jit(solution)/shard_map/prepare/pallas_call | solution.py:233
  33.5 0.0 copy-start
  33.5 0.0 copy-done.1
  33.5 68.6 %exchange.2 = (f32[64,176,128]{2,1,0:T(8,128)}, s32[1,128]{1,0:T(1,128)}, f32[16384,128]{1,0:T(8,128)}) custom-call(s32[64,4,128]{2,1,0:T(4,128)} %get-tuple-element.66.req_ref, f32[16,64,512]{2,1,0:T(8,128)S(1)} %get-tuple-element.151.tab_ref, s32[128,128]{1,0:T(8,128)} %get-tuple-element.68.epoch_ref, f32[128,128]{1,0:T(8,128)S(1)} %bitcast.24, ...), custom_call_target="tpu_custom_call" | custom-call | tf_op jit(solution)/shard_map/exchange/pallas_call | solution.py:369
  102.2 0.0 copy-done
  102.2 0.0 copy-start.2
  102.2 0.0 copy-start.3
  102.2 0.0 copy-start.4
  102.2 41.0 %join.2 = f32[32,64,384]{2,1,0:T(8,128)S(1)} custom-call(s32[128,128]{1,0:T(8,128)} %get-tuple-element.70.line_ref, s32[64,128]{1,0:T(8,128)} %get-tuple-element.71.span_ref, f32[11264,128]{1,0:T(8,128)} %bitcast.22, f32[16384,128]{1,0:T(8,128)} %get-tuple-element.73.sorted_ref), custom_call_target="tpu_custom_call" | custom-call | tf_op jit(solution)/shard_map/join/pallas_call | solution.py:469
  143.2 0.0 copy-done.2
  143.3 0.0 copy-done.3
  143.3 0.0 copy-done.4
  143.3 0.8 while.12
  144.0 38.6 %reduce_factor.1 = f32[4,192,192]{2,1,0:T(8,128)} custom-call(f32[8,4,64,384]{3,2,1,0:T(8,128)S(1)} %bitcast.17), custom_call_target="tpu_custom_call" | custom-call | tf_op jit(solution)/shard_map/reduce_factor/pallas_call | solution.py:603
  182.7 2.1 %copy.21 = f32[1,4,192,192]{3,2,1,0:T(8,128)} copy(f32[1,4,192,192]{3,2,1,0:T(8,128)} %bitcast.23) | data formatting | bytes 1179648
Async XLA Ops:
  0.0 33.5 %copy-start.1 = (f32[1,16384]{1,0:T(1,128)S(1)}, f32[1,16384]{1,0:T(1,128)}, u32[]{:S(2)}) copy-start(f32[1,16384]{1,0:T(1,128)} %param.10) | copy-start | bytes 196612
  33.5 68.7 %copy-start = (f32[16,64,512]{2,1,0:T(8,128)}, f32[16,64,512]{2,1,0:T(8,128)S(1)}, u32[]{:S(2)}) copy-start(f32[16,64,512]{2,1,0:T(8,128)S(1)} %get-tuple-element.151.tab_ref) | copy-start | bytes 6291460
  102.2 41.0 %copy-start.2 = (s32[1,16384,1]{1,2,0:T(1,128)S(1)}, s32[1,16384,1]{1,2,0:T(1,128)}, u32[]{:S(2)}) copy-start(s32[1,16384,1]{1,2,0:T(1,128)} %param.11) | copy-start | bytes 196612
  102.2 41.0 %copy-start.3 = (s32[1,16384]{1,0:T(1,128)S(1)}, s32[1,16384]{1,0:T(1,128)}, u32[]{:S(2)}) copy-start(s32[1,16384]{1,0:T(1,128)} %param.12) | copy-start | bytes 196612
  102.2 41.0 %copy-start.4 = (s32[1,16384,1]{1,2,0:T(1,128)S(1)}, s32[1,16384,1]{1,2,0:T(1,128)}, u32[]{:S(2)}) copy-start(s32[1,16384,1]{1,2,0:T(1,128)} %param.13) | copy-start | bytes 196612
